TPU v7x, 128 devices: a whole 4x4x4 slice. The times are simulated.
128 devices in a mesh: seq: 16 (over x_lo, y, core), head: 8 (over z, x_hi).
Axes of the slice: x: 4 (x_hi: 2, x_lo: 2; x = x_hi * 2 + x_lo), y: 4, z: 4, core: 2. Of those that a mesh axis runs over, the one named last changes fastest.
Arguments:
- queries: bfloat16 [16384, 4096], P('seq', 'head'), may hold values from -6 to 6
- key_states: bfloat16 [16384, 2048], P('seq', 'head'), may hold values from -6 to 6
- value_states: bfloat16 [16384, 2048], P('seq', 'head'), may hold values from -6 to 6
- outputs: bfloat16 [16384, 4096], P('seq', 'head'), may hold values from -6 to 6
- out_grad: bfloat16 [16384, 4096], P(('seq', 'head')), may hold values from -96 to 96
- log_norm: float32 [32, 16384], P('head', 'seq'), may hold values from 6 to 7.6
Outputs:
- query_grad: bfloat16 [16384, 4096], P(('seq', 'head'))
- key_grad: bfloat16 [16384, 2048], P(('seq', 'head'))
- value_grad: bfloat16 [16384, 2048], P(('seq', 'head'))
All inputs are finite; a program needn't handle non-finite values.
Results may differ from a plain program's by a relative error of at most 0.0049.
Values may be sent and summed in bfloat16 or wider, within the bound.
No kernel may reach another device: no remote copies, remote signals or barrier semaphores. Data moves between devices by JAX's collectives and lax.ppermute only.
A program may use at most 128 MiB of HBM per device.

v0:
```python
import jax
import jax.numpy as jnp
from jax import lax
from jax.sharding import PartitionSpec as P

HEAD_DIM = 128
WINDOW = 1024


score_scale = 168.0 ** (-0.5)


def from_behind(shard, axis, by):
    devices = lax.axis_size(axis)
    pairs = [(i, i + by) for i in range(devices) if 0 <= i + by < devices]
    return lax.ppermute(shard, axis, pairs)


def band_tile(
    q_rows, grad_rows, norm_rows, delta_rows, key_rows, value_rows, query_start, key_start
):
    row_count = q_rows.shape[0]
    key_count = key_rows.shape[0]
    key_heads = key_rows.shape[1] // HEAD_DIM
    query_heads = q_rows.shape[1] // HEAD_DIM
    group_size = query_heads // key_heads
    query_split = q_rows.reshape(row_count, key_heads, group_size, HEAD_DIM)
    grad_split = grad_rows.reshape(row_count, key_heads, group_size, HEAD_DIM)
    key_split = key_rows.reshape(key_count, key_heads, HEAD_DIM)
    value_split = value_rows.reshape(key_count, key_heads, HEAD_DIM)
    scores = (
        jnp.einsum("qhgd,khd->hgqk", query_split, key_split, preferred_element_type=jnp.float32)
        * score_scale
    )
    query_pos = query_start + lax.broadcasted_iota(jnp.int32, (row_count, key_count), 0)
    key_pos = key_start + lax.broadcasted_iota(jnp.int32, (row_count, key_count), 1)
    offset_gap = query_pos - key_pos
    allowed = (offset_gap >= 0) & (offset_gap < WINDOW) & (key_pos >= 0)
    norm_split = norm_rows.reshape(key_heads, group_size, row_count)
    delta_split = delta_rows.reshape(key_heads, group_size, row_count)
    probability = jnp.where(allowed, jnp.exp(scores - norm_split[..., None]), 0.0)
    probs_low = probability.astype(jnp.bfloat16)
    grad_prob = jnp.einsum(
        "qhgd,khd->hgqk", grad_split, value_split, preferred_element_type=jnp.float32
    )
    grad_score = (probability * (grad_prob - delta_split[..., None])).astype(jnp.bfloat16)
    grad_q = (
        jnp.einsum("hgqk,khd->qhgd", grad_score, key_split, preferred_element_type=jnp.float32)
        * score_scale
    )
    grad_k = (
        jnp.einsum("hgqk,qhgd->khd", grad_score, query_split, preferred_element_type=jnp.float32)
        * score_scale
    )
    grad_v = jnp.einsum("hgqk,qhgd->khd", probs_low, grad_split, preferred_element_type=jnp.float32)
    return (
        grad_q.reshape(row_count, query_heads * HEAD_DIM),
        grad_k.reshape(key_count, key_heads * HEAD_DIM),
        grad_v.reshape(key_count, key_heads * HEAD_DIM),
    )


def on_device(queries, key_states, value_states, outputs, out_grad, log_norm):
    local_tokens = queries.shape[0]
    query_heads = queries.shape[1] // HEAD_DIM
    key_width = key_states.shape[1]
    block_rows = min(512, local_tokens)
    block_count = local_tokens // block_rows
    span_rows = WINDOW + block_rows
    base_pos = lax.axis_index("seq") * local_tokens
    grad_local = lax.all_to_all(out_grad, "head", split_axis=1, concat_axis=0, tiled=True)
    grad_delta = jnp.einsum(
        "qhd,qhd->hq",
        grad_local.reshape(local_tokens, query_heads, HEAD_DIM),
        outputs.reshape(local_tokens, query_heads, HEAD_DIM),
        preferred_element_type=jnp.float32,
    )
    key_rim, value_rim = from_behind((key_states, value_states), "seq", 1)
    key_ext = jnp.concatenate([key_rim, key_states], 0)
    value_ext = jnp.concatenate([value_rim, value_states], 0)

    def one_block(block_index, carried):
        grad_q_all, grad_k_all, grad_v_all = carried
        row_start = block_index * block_rows
        q_rows = lax.dynamic_slice_in_dim(queries, row_start, block_rows, 0)
        grad_rows = lax.dynamic_slice_in_dim(grad_local, row_start, block_rows, 0)
        norm_rows = lax.dynamic_slice_in_dim(log_norm, row_start, block_rows, 1)
        delta_rows = lax.dynamic_slice_in_dim(grad_delta, row_start, block_rows, 1)
        key_rows = lax.dynamic_slice_in_dim(key_ext, row_start, span_rows, 0)
        value_rows = lax.dynamic_slice_in_dim(value_ext, row_start, span_rows, 0)
        grad_q, grad_k, grad_v = band_tile(
            q_rows,
            grad_rows,
            norm_rows,
            delta_rows,
            key_rows,
            value_rows,
            base_pos + row_start,
            base_pos + row_start - WINDOW,
        )
        grad_q_all = lax.dynamic_update_slice_in_dim(
            grad_q_all, grad_q.astype(jnp.bfloat16), row_start, 0
        )
        old_k = lax.dynamic_slice_in_dim(grad_k_all, row_start, span_rows, 0)
        old_v = lax.dynamic_slice_in_dim(grad_v_all, row_start, span_rows, 0)
        grad_k_all = lax.dynamic_update_slice_in_dim(grad_k_all, old_k + grad_k, row_start, 0)
        grad_v_all = lax.dynamic_update_slice_in_dim(grad_v_all, old_v + grad_v, row_start, 0)
        return (grad_q_all, grad_k_all, grad_v_all)

    initial = (
        jnp.zeros((local_tokens, queries.shape[1]), jnp.bfloat16),
        jnp.zeros((WINDOW + local_tokens, key_width), jnp.float32),
        jnp.zeros((WINDOW + local_tokens, key_width), jnp.float32),
    )
    grad_q_all, grad_k_all, grad_v_all = lax.fori_loop(0, block_count, one_block, initial)
    rim_k, rim_v = from_behind((grad_k_all[:WINDOW], grad_v_all[:WINDOW]), "seq", -1)
    own_k = grad_k_all[WINDOW:].at[local_tokens - WINDOW :].add(rim_k).astype(jnp.bfloat16)
    own_v = grad_v_all[WINDOW:].at[local_tokens - WINDOW :].add(rim_v).astype(jnp.bfloat16)
    query_grad, key_grad, value_grad = (
        lax.all_to_all(grad_q_all, "head", split_axis=0, concat_axis=1, tiled=True),
        lax.all_to_all(own_k, "head", split_axis=0, concat_axis=1, tiled=True),
        lax.all_to_all(own_v, "head", split_axis=0, concat_axis=1, tiled=True),
    )
    return (query_grad, key_grad, value_grad)


def solution(mesh):
    placed = (
        P("seq", "head"),
        P("seq", "head"),
        P("seq", "head"),
        P("seq", "head"),
        P(("seq", "head"), None),
        P("head", "seq"),
    )
    return jax.shard_map(
        on_device,
        mesh=mesh,
        in_specs=placed,
        out_specs=(P(("seq", "head"), None), P(("seq", "head"), None), P(("seq", "head"), None)),
        check_vma=False,
    )
```

profile of v0, /device:TPU:2, one launch (start us, length us, event | category | flops | bytes accessed | tf_op | source)
XLA Modules:
  0.0 199.4 jit_solution(5024576055303834616)
XLA Ops:
  0.6 1.3 copy.58
  1.9 1.9 collective-permute-start
  3.9 2.3 %copy.62 = bf16[128,4096]{0,1:T(8,128)(2,1)} copy(bf16[128,4096]{1,0:T(8,128)(2,1)} %param.20) | data formatting | bytes 2097152 | tf_op args[4]
  6.1 6.9 %all-to-all-start = ((bf16[128,8,512]{0,2,1:T(8,128)(2,1)}), bf16[128,8,512]{0,2,1:T(8,128)(2,1)S(1)}, u32[]{:S(2)}, u32[]{:S(2)}) async-start(bf16[128,8,512]{0,2,1:T(8,128)(2,1)} %bitcast.22), calls=%async_computation | async-start | bytes 2097152 | tf_op jit(solution)/shard_map/all_to_all | solution.py:71
  13.2 3.3 %collective-permute-start.1 = (bf16[1024,256]{0,1:T(8,128)(2,1)S(1)}, bf16[1024,256]{0,1:T(8,128)(2,1)}, u32[]{:S(2)}, u32[]{:S(2)}) collective-permute-start(bf16[1024,256]{0,1:T(8,128)(2,1)S(1)} %copy.60), channel_id=1, source_target_pairs={{0,8},{8,16},{16,24},{24,32},{32,40},{40,48},{48,56},{56,64},{64,7... | collective-permute-start | bytes 1572872 | tf_op jit(solution)/shard_map/ppermute | solution.py:16
  16.6 1.3 reshape.153
  17.9 2.1 %pad_maximum_fusion = bf16[2048,256]{0,1:T(8,128)(2,1)} fusion(bf16[1024,256]{0,1:T(8,128)(2,1)S(1)} %copy.58, bf16[1024,256]{0,1:T(8,128)(2,1)} %collective-permute-done), kind=kLoop, calls=%fused_computation.34 | loop fusion | flops 2097152 | bytes 2097152 | tf_op jit(solution)/shard_map/concatenate | solution.py:79
  20.0 15.8 %collective-permute-done.1 = bf16[1024,256]{0,1:T(8,128)(2,1)} collective-permute-done((bf16[1024,256]{0,1:T(8,128)(2,1)S(1)}, bf16[1024,256]{0,1:T(8,128)(2,1)}, u32[]{:S(2)}, u32[]{:S(2)}) %collective-permute-start.1) | collective-permute-done | bytes 524320 | tf_op jit(solution)/shard_map/ppermute | solution.py:16
  35.8 2.1 %pad_maximum_fusion.1 = bf16[2048,256]{0,1:T(8,128)(2,1)} fusion(bf16[1024,256]{0,1:T(8,128)(2,1)S(1)} %copy.60, bf16[1024,256]{0,1:T(8,128)(2,1)} %collective-permute-done.1), kind=kLoop, calls=%fused_computation.35 | loop fusion | flops 2097152 | bytes 2097152 | tf_op jit(solution)/shard_map/concatenate | solution.py:80
  37.9 1.6 copy.64
  39.6 1.5 reshape.152
  41.1 1.6 bitcast_convert_fusion
  42.7 2.9 %copy.91 = f32[4,1024,128]{2,0,1:T(4,128)} copy(f32[4,1024,128]{1,2,0:T(8,128)} %bitcast_convert_fusion) | data formatting | bytes 4194304
  45.5 2.8 %multiply_reduce_fusion = f32[4,1024]{0,1:T(8,128)S(1)} fusion(f32[4,1024,128]{2,0,1:T(4,128)} %copy.91, bf16[1024,4,128]{2,1,0:T(4,128)(2,1)S(1)} %reshape.153), kind=kLoop, calls=%fused_computation.33 | loop fusion | flops 1568768 | bytes 3162112
  48.5 1.3 copy.63
  49.8 1.0 broadcast_in_dim.25.clone
  51.1 1.5 broadcast.135.clone
  52.6 83.2 %while.23 = (s32[]{:T(128)}, bf16[1024,512]{1,0:T(8,128)(2,1)}, f32[2048,256]{0,1:T(8,128)S(1)}, f32[2048,256]{0,1:T(8,128)}, bf16[2048,256]{0,1:T(8,128)(2,1)},...) while((s32[]{:T(128)}, bf16[1024,512]{1,0:T(8,128)(2,1)}, ...), condition=%wide.region_1.2_spmd, body=%wide.region_0.1_spmd.sunk | while | flops 4063630336 | bytes 158445072 | solution.py:115
  52.6 1.2 constant_dynamic-slice_fusion.12
  53.8 1.9 constant_dynamic-slice_fusion.13
  55.7 1.3 copy.105
  57.0 6.4 %fusion.50 = f32[2,1536,512,2]{2,1,3,0:T(8,128)} fusion(bf16[1536,2,128,1]{0,2,3,1:T(8,128)(2,1)S(1)} %bitcast.121, bf16[512,2,2,128]{0,3,2,1:T(8,128)(2,1)S(1)} %bitcast.123), kind=kOutput, calls=%fused_computation.39.clone.1 | convolution fusion | flops 805306368 | bytes 13893632 | tf_op jit(solution)/shard_map/while/body/eval_jaxpr/qhgd,khd->hgqk/dot_general | solution.py:32
  63.3 1.0 constant_dynamic-slice_fusion.14
  65.2 2.0 %copy.106 = bf16[512,512]{0,1:T(8,128)(2,1)} copy(bf16[512,512]{1,0:T(8,128)(2,1)} %constant_dynamic-slice_fusion.15) | data formatting | bytes 1048576 | tf_op jit(solution)/shard_map/while/body/eval_jaxpr/dynamic_slice | solution.py:86
  67.3 1.2 fusion.51
  68.5 9.5 %fusion.52 = bf16[2,2,512,1536]{2,3,1,0:T(8,128)(2,1)S(1)} fusion(f32[2,1536,512,2]{2,1,3,0:T(8,128)} %fusion.50, bf16[1536,2,128,1]{0,2,3,1:T(8,128)(2,1)} %bitcast.126, bf16[512,2,2,128]{0,3,2,1:T(8,128)(2,1)} %bitcast.127, f32[2,2,512]{2,1,0:T(2,128)S(1)} %sub.125, f32[2,2,512]{2,1,0:T(2,128)S(1)} %sub.126, pred[512,1536]{0,1:T(8,128)(4,1)S(1)} %fusion.51), kind=kOutput, calls=%fused_computation.2.clone.1 | convolution fusion | flops 824180736 | bytes 20987904 | tf_op jit(solution)/shard_map/while/body/eval_jaxpr/qhgd,khd->hgqk/dot_general | solution.py:43
  78.1 2.3 %fusion.53 = bf16[2,128,2,512]{3,1,2,0:T(8,128)(2,1)} fusion(bf16[1536,2,128,1]{0,2,3,1:T(8,128)(2,1)S(1)} %bitcast.122, bf16[2,2,512,1536]{2,3,1,0:T(8,128)(2,1)S(1)} %fusion.52), kind=kOutput, calls=%fused_computation.18.clone.1 | convolution fusion | flops 805830656 | bytes 7602176 | tf_op jit(solution)/shard_map/while/body/eval_jaxpr/hgqk,khd->qhgd/dot_general | solution.py:48
  80.8 1.3 copy.107
  82.9 7.0 %fusion.54 = f32[2,128,1536,1]{2,1,3,0:T(8,128)S(1)} fusion(bf16[512,2,2,128]{0,3,2,1:T(8,128)(2,1)} %bitcast.128, f32[2,1536,512,2]{2,1,3,0:T(8,128)} %fusion.50, f32[2,2,512]{2,1,0:T(2,128)S(1)} %sub.126, pred[512,1536]{0,1:T(8,128)(4,1)} %copy-done.4), kind=kOutput, calls=%fused_computation.7.clone.1 | convolution fusion | flops 817889280 | bytes 15474688 | tf_op jit(solution)/shard_map/while/body/eval_jaxpr/hgqk,qhgd->khd/dot_general | solution.py:55
  89.9 2.2 %fusion.55 = f32[2,128,1536]{2,1,0:T(8,128)S(1)} fusion(bf16[512,2,2,128]{0,3,2,1:T(8,128)(2,1)S(1)} %bitcast.124, bf16[2,2,512,1536]{2,3,1,0:T(8,128)(2,1)S(1)} %bitcast.120), kind=kOutput, calls=%fused_computation.14.clone.1 | convolution fusion | flops 805699584 | bytes 8388608 | tf_op jit(solution)/shard_map/while/body/eval_jaxpr/hgqk,qhgd->khd/dot_general | solution.py:52
  92.1 0.8 constant_dynamic-update-slice_fusion.6
  92.9 1.3 copy-done.2
  94.2 1.2 constant_dynamic-slice_fusion.12
  95.4 1.9 constant_dynamic-slice_fusion.13
  97.3 1.3 copy.105
  98.6 6.4 %fusion.50 = f32[2,1536,512,2]{2,1,3,0:T(8,128)} fusion(bf16[1536,2,128,1]{0,2,3,1:T(8,128)(2,1)S(1)} %bitcast.121, bf16[512,2,2,128]{0,3,2,1:T(8,128)(2,1)S(1)} %bitcast.123), kind=kOutput, calls=%fused_computation.39.clone.1 | convolution fusion | flops 805306368 | bytes 13893632 | tf_op jit(solution)/shard_map/while/body/eval_jaxpr/qhgd,khd->hgqk/dot_general | solution.py:32
  104.9 1.0 constant_dynamic-slice_fusion.14
  106.8 2.0 %copy.106 = bf16[512,512]{0,1:T(8,128)(2,1)} copy(bf16[512,512]{1,0:T(8,128)(2,1)} %constant_dynamic-slice_fusion.15) | data formatting | bytes 1048576 | tf_op jit(solution)/shard_map/while/body/eval_jaxpr/dynamic_slice | solution.py:86
  108.9 1.2 fusion.51
  110.1 9.5 %fusion.52 = bf16[2,2,512,1536]{2,3,1,0:T(8,128)(2,1)S(1)} fusion(f32[2,1536,512,2]{2,1,3,0:T(8,128)} %fusion.50, bf16[1536,2,128,1]{0,2,3,1:T(8,128)(2,1)} %bitcast.126, bf16[512,2,2,128]{0,3,2,1:T(8,128)(2,1)} %bitcast.127, f32[2,2,512]{2,1,0:T(2,128)S(1)} %sub.125, f32[2,2,512]{2,1,0:T(2,128)S(1)} %sub.126, pred[512,1536]{0,1:T(8,128)(4,1)S(1)} %fusion.51), kind=kOutput, calls=%fused_computation.2.clone.1 | convolution fusion | flops 824180736 | bytes 20987904 | tf_op jit(solution)/shard_map/while/body/eval_jaxpr/qhgd,khd->hgqk/dot_general | solution.py:43
  119.7 2.3 %fusion.53 = bf16[2,128,2,512]{3,1,2,0:T(8,128)(2,1)} fusion(bf16[1536,2,128,1]{0,2,3,1:T(8,128)(2,1)S(1)} %bitcast.122, bf16[2,2,512,1536]{2,3,1,0:T(8,128)(2,1)S(1)} %fusion.52), kind=kOutput, calls=%fused_computation.18.clone.1 | convolution fusion | flops 805830656 | bytes 7602176 | tf_op jit(solution)/shard_map/while/body/eval_jaxpr/hgqk,khd->qhgd/dot_general | solution.py:48
  122.4 1.3 copy.107
  124.5 7.0 %fusion.54 = f32[2,128,1536,1]{2,1,3,0:T(8,128)S(1)} fusion(bf16[512,2,2,128]{0,3,2,1:T(8,128)(2,1)} %bitcast.128, f32[2,1536,512,2]{2,1,3,0:T(8,128)} %fusion.50, f32[2,2,512]{2,1,0:T(2,128)S(1)} %sub.126, pred[512,1536]{0,1:T(8,128)(4,1)} %copy-done.4), kind=kOutput, calls=%fused_computation.7.clone.1 | convolution fusion | flops 817889280 | bytes 15474688 | tf_op jit(solution)/shard_map/while/body/eval_jaxpr/hgqk,qhgd->khd/dot_general | solution.py:55
  131.5 2.2 %fusion.55 = f32[2,128,1536]{2,1,0:T(8,128)S(1)} fusion(bf16[512,2,2,128]{0,3,2,1:T(8,128)(2,1)S(1)} %bitcast.124, bf16[2,2,512,1536]{2,3,1,0:T(8,128)(2,1)S(1)} %bitcast.120), kind=kOutput, calls=%fused_computation.14.clone.1 | convolution fusion | flops 805699584 | bytes 8388608 | tf_op jit(solution)/shard_map/while/body/eval_jaxpr/hgqk,qhgd->khd/dot_general | solution.py:52
  134.5 1.3 copy-done.2
  135.8 1.1 slice.41
  136.9 1.9 collective-permute-start.2
  138.8 6.4 %all-to-all-start.1 = ((bf16[8,128,512]{2,1,0:T(8,128)(2,1)}), bf16[8,128,512]{2,1,0:T(8,128)(2,1)S(1)}, u32[]{:S(2)}, u32[]{:S(2)}) async-start(bf16[8,128,512]{2,1,0:T(8,128)(2,1)} %bitcast.131), calls=%async_computation.1 | async-start | bytes 2097152 | tf_op jit(solution)/shard_map/all_to_all | solution.py:120
  145.3 2.3 %slice.43 = f32[1024,256]{0,1:T(8,128)} slice(f32[2048,256]{0,1:T(8,128)} %get-tuple-element.311), slice={[0:1024], [0:256]} | slice | bytes 2097152 | tf_op jit(solution)/shard_map/slice | solution.py:116
  147.6 1.9 collective-permute-start.3
  149.5 7.2 %collective-permute-done.2 = f32[1024,256]{0,1:T(8,128)} collective-permute-done((f32[1024,256]{0,1:T(8,128)}, f32[1024,256]{0,1:T(8,128)}, u32[]{:S(2)}, u32[]{:S(2)}) %collective-permute-start.2) | collective-permute-done | bytes 1048608 | tf_op jit(solution)/shard_map/ppermute | solution.py:16
  156.7 2.2 %add_convert_fusion.1 = bf16[1024,256]{0,1:T(8,128)(2,1)} fusion(f32[1024,256]{0,1:T(8,128)} %collective-permute-done.2, f32[2048,256]{0,1:T(8,128)S(1)} %get-tuple-element.310), kind=kLoop, calls=%fused_computation.38 | loop fusion | flops 524288 | bytes 2621440 | tf_op jit(solution)/shard_map/convert_element_type | solution.py:117
  158.9 2.0 %copy.69 = bf16[1024,256]{1,0:T(8,128)(2,1)} copy(bf16[1024,256]{0,1:T(8,128)(2,1)} %add_convert_fusion.1) | data formatting | bytes 1048576 | tf_op jit(solution)/shard_map/convert_element_type | solution.py:117
  160.9 6.7 %all-to-all-done.1 = bf16[8,128,512]{2,1,0:T(8,128)(2,1)S(1)} async-done(((bf16[8,128,512]{2,1,0:T(8,128)(2,1)}), bf16[8,128,512]{2,1,0:T(8,128)(2,1)S(1)}, u32[]{:S(2)}, u32[]{:S(2)}) %all-to-all-start.1) | async-done | bytes 1048608 | tf_op jit(solution)/shard_map/all_to_all | solution.py:120
  167.6 3.5 %all-to-all-start.2 = ((bf16[8,128,256]{2,1,0:T(8,128)(2,1)}), bf16[8,128,256]{2,1,0:T(8,128)(2,1)S(1)}, u32[]{:S(2)}, u32[]{:S(2)}) async-start(bf16[8,128,256]{2,1,0:T(8,128)(2,1)} %bitcast.29), calls=%async_computation.2 | async-start | bytes 1048576 | tf_op jit(solution)/shard_map/all_to_all | solution.py:121
  171.1 5.6 %collective-permute-done.3 = f32[1024,256]{0,1:T(8,128)} collective-permute-done((f32[1024,256]{0,1:T(8,128)}, f32[1024,256]{0,1:T(8,128)}, u32[]{:S(2)}, u32[]{:S(2)}) %collective-permute-start.3) | collective-permute-done | bytes 1048608 | tf_op jit(solution)/shard_map/ppermute | solution.py:16
  176.7 1.7 add_convert_fusion
  178.4 1.0 copy.71
  179.4 5.1 %all-to-all-done.2 = bf16[8,128,256]{2,1,0:T(8,128)(2,1)S(1)} async-done(((bf16[8,128,256]{2,1,0:T(8,128)(2,1)}), bf16[8,128,256]{2,1,0:T(8,128)(2,1)S(1)}, u32[]{:S(2)}, u32[]{:S(2)}) %all-to-all-start.2) | async-done | bytes 524320 | tf_op jit(solution)/shard_map/all_to_all | solution.py:121
  184.5 3.5 %all-to-all-start.3 = ((bf16[8,128,256]{2,1,0:T(8,128)(2,1)}), bf16[8,128,256]{2,1,0:T(8,128)(2,1)S(1)}, u32[]{:S(2)}, u32[]{:S(2)}) async-start(bf16[8,128,256]{2,1,0:T(8,128)(2,1)} %bitcast.32), calls=%async_computation.3 | async-start | bytes 1048576 | tf_op jit(solution)/shard_map/all_to_all | solution.py:122
  188.7 1.3 copy.73
  190.3 1.0 copy.74
  191.3 6.9 %all-to-all-done.3 = bf16[8,128,256]{2,1,0:T(8,128)(2,1)S(1)} async-done(((bf16[8,128,256]{2,1,0:T(8,128)(2,1)}), bf16[8,128,256]{2,1,0:T(8,128)(2,1)S(1)}, u32[]{:S(2)}, u32[]{:S(2)}) %all-to-all-start.3) | async-done | bytes 524320 | tf_op jit(solution)/shard_map/all_to_all | solution.py:122
  198.4 1.0 copy.75
  (63 shorter events, 7.1 us)
Async XLA Ops:
  0.6 12.4 %copy-start.6 = (bf16[1024,256]{1,0:T(8,128)(2,1)S(1)}, bf16[1024,256]{1,0:T(8,128)(2,1)}, u32[]{:S(2)}) copy-start(bf16[1024,256]{1,0:T(8,128)(2,1)} %param.18) | copy-start | bytes 1572868
  1.9 16.0 %collective-permute-start = (bf16[1024,256]{0,1:T(8,128)(2,1)S(1)}, bf16[1024,256]{0,1:T(8,128)(2,1)}, u32[]{:S(2)}, u32[]{:S(2)}) collective-permute-start(bf16[1024,256]{0,1:T(8,128)(2,1)S(1)} %copy.58), channel_id=1, source_target_pairs={{0,8},{8,16},{16,24},{24,32},{32,40},{40,48},{48,56},{56,64},{64,7... | collective-permute-start | bytes 1572872 | tf_op jit(solution)/shard_map/ppermute | solution.py:16
  6.1 31.8 %all-to-all-start = ((bf16[128,8,512]{0,2,1:T(8,128)(2,1)}), bf16[128,8,512]{0,2,1:T(8,128)(2,1)S(1)}, u32[]{:S(2)}, u32[]{:S(2)}) async-start(bf16[128,8,512]{0,2,1:T(8,128)(2,1)} %bitcast.22), calls=%async_computation | async-start | bytes 2097152 | tf_op jit(solution)/shard_map/all_to_all | solution.py:71
  13.2 22.6 %collective-permute-start.1 = (bf16[1024,256]{0,1:T(8,128)(2,1)S(1)}, bf16[1024,256]{0,1:T(8,128)(2,1)}, u32[]{:S(2)}, u32[]{:S(2)}) collective-permute-start(bf16[1024,256]{0,1:T(8,128)(2,1)S(1)} %copy.60), channel_id=1, source_target_pairs={{0,8},{8,16},{16,24},{24,32},{32,40},{40,48},{48,56},{56,64},{64,7... | collective-permute-start | bytes 1572872 | tf_op jit(solution)/shard_map/ppermute | solution.py:16
  49.8 2.8 %copy-start.7 = (f32[4,1024]{1,0:T(4,128)S(1)}, f32[4,1024]{1,0:T(4,128)}, u32[]{:S(2)}) copy-start(f32[4,1024]{1,0:T(4,128)} %param.21) | copy-start | bytes 49156
  57.0 6.4 %copy-start.3 = (bf16[2048,256]{0,1:T(8,128)(2,1)S(1)}, bf16[2048,256]{0,1:T(8,128)(2,1)}, u32[]{:S(2)}) copy-start(bf16[2048,256]{0,1:T(8,128)(2,1)} %get-tuple-element.485) | copy-start | bytes 3145732 | tf_op jit(solution)/shard_map/while
  57.0 7.4 %copy-start.5 = (bf16[1024,512]{1,0:T(8,128)(2,1)S(1)}, bf16[1024,512]{1,0:T(8,128)(2,1)}, u32[]{:S(2)}) copy-start(bf16[1024,512]{1,0:T(8,128)(2,1)} %get-tuple-element.486) | copy-start | bytes 3145732 | tf_op jit(solution)/shard_map/while
  68.5 9.5 %copy-start.4 = (pred[512,1536]{0,1:T(8,128)(4,1)}, pred[512,1536]{0,1:T(8,128)(4,1)S(1)}, u32[]{:S(2)}) copy-start(pred[512,1536]{0,1:T(8,128)(4,1)S(1)} %fusion.51) | copy-start | bytes 2359300 | tf_op jit(solution)/shard_map/while
  78.1 2.7 %copy-start = (bf16[2,2,512,1536]{2,3,1,0:T(8,128)(2,1)}, bf16[2,2,512,1536]{2,3,1,0:T(8,128)(2,1)S(1)}, u32[]{:S(2)}) copy-start(bf16[2,2,512,1536]{2,3,1,0:T(8,128)(2,1)S(1)} %fusion.52) | copy-start | bytes 18874372 | tf_op jit(solution)/shard_map/while
  82.0 7.8 %slice-start = ((s8[6291456]{0:T(1024)(128)(4,1)}), s8[4194304]{0:T(1024)(128)(4,1)S(1)}, s32[]{:S(2)}) async-start(s8[6291456]{0:T(1024)(128)(4,1)} %bitcast.119), calls=%async_computation.4 | async-start | bytes 8388608 | tf_op jit(solution)/shard_map/while
  82.9 7.0 %slice-start.1 = ((s8[6291456]{0:T(1024)(128)(4,1)}), s8[2097152]{0:T(1024)(128)(4,1)S(1)}, s32[]{:S(2)}) async-start(s8[6291456]{0:T(1024)(128)(4,1)} %bitcast.119), calls=%async_computation.5 | async-start | bytes 4194304 | tf_op jit(solution)/shard_map/while
  89.9 2.2 %copy-start.1 = (f32[2048,256]{0,1:T(8,128)S(1)}, f32[2048,256]{0,1:T(8,128)}, u32[]{:S(2)}) copy-start(f32[2048,256]{0,1:T(8,128)} %get-tuple-element.463) | copy-start | bytes 6291460 | tf_op jit(solution)/shard_map/while
  92.9 1.3 copy-start.2
  98.6 6.4 %copy-start.3 = (bf16[2048,256]{0,1:T(8,128)(2,1)S(1)}, bf16[2048,256]{0,1:T(8,128)(2,1)}, u32[]{:S(2)}) copy-start(bf16[2048,256]{0,1:T(8,128)(2,1)} %get-tuple-element.485) | copy-start | bytes 3145732 | tf_op jit(solution)/shard_map/while
  98.6 7.4 %copy-start.5 = (bf16[1024,512]{1,0:T(8,128)(2,1)S(1)}, bf16[1024,512]{1,0:T(8,128)(2,1)}, u32[]{:S(2)}) copy-start(bf16[1024,512]{1,0:T(8,128)(2,1)} %get-tuple-element.486) | copy-start | bytes 3145732 | tf_op jit(solution)/shard_map/while
  110.1 9.5 %copy-start.4 = (pred[512,1536]{0,1:T(8,128)(4,1)}, pred[512,1536]{0,1:T(8,128)(4,1)S(1)}, u32[]{:S(2)}) copy-start(pred[512,1536]{0,1:T(8,128)(4,1)S(1)} %fusion.51) | copy-start | bytes 2359300 | tf_op jit(solution)/shard_map/while
  119.7 2.7 %copy-start = (bf16[2,2,512,1536]{2,3,1,0:T(8,128)(2,1)}, bf16[2,2,512,1536]{2,3,1,0:T(8,128)(2,1)S(1)}, u32[]{:S(2)}) copy-start(bf16[2,2,512,1536]{2,3,1,0:T(8,128)(2,1)S(1)} %fusion.52) | copy-start | bytes 18874372 | tf_op jit(solution)/shard_map/while
  123.6 7.8 %slice-start = ((s8[6291456]{0:T(1024)(128)(4,1)}), s8[4194304]{0:T(1024)(128)(4,1)S(1)}, s32[]{:S(2)}) async-start(s8[6291456]{0:T(1024)(128)(4,1)} %bitcast.119), calls=%async_computation.4 | async-start | bytes 8388608 | tf_op jit(solution)/shard_map/while
  124.5 7.0 %slice-start.1 = ((s8[6291456]{0:T(1024)(128)(4,1)}), s8[2097152]{0:T(1024)(128)(4,1)S(1)}, s32[]{:S(2)}) async-start(s8[6291456]{0:T(1024)(128)(4,1)} %bitcast.119), calls=%async_computation.5 | async-start | bytes 4194304 | tf_op jit(solution)/shard_map/while
  131.5 2.2 %copy-start.1 = (f32[2048,256]{0,1:T(8,128)S(1)}, f32[2048,256]{0,1:T(8,128)}, u32[]{:S(2)}) copy-start(f32[2048,256]{0,1:T(8,128)} %get-tuple-element.463) | copy-start | bytes 6291460 | tf_op jit(solution)/shard_map/while
  134.5 1.3 copy-start.2
  136.9 19.8 %collective-permute-start.2 = (f32[1024,256]{0,1:T(8,128)}, f32[1024,256]{0,1:T(8,128)}, u32[]{:S(2)}, u32[]{:S(2)}) collective-permute-start(f32[1024,256]{0,1:T(8,128)} %slice.41), channel_id=1, source_target_pairs={{8,0},{16,8},{24,16},{32,24},{40,32},{48,40},{56,48},{64,56},{72,6... | collective-permute-start | bytes 3145736 | tf_op jit(solution)/shard_map/ppermute | solution.py:16
  138.8 28.7 %all-to-all-start.1 = ((bf16[8,128,512]{2,1,0:T(8,128)(2,1)}), bf16[8,128,512]{2,1,0:T(8,128)(2,1)S(1)}, u32[]{:S(2)}, u32[]{:S(2)}) async-start(bf16[8,128,512]{2,1,0:T(8,128)(2,1)} %bitcast.131), calls=%async_computation.1 | async-start | bytes 2097152 | tf_op jit(solution)/shard_map/all_to_all | solution.py:120
  147.6 29.2 %collective-permute-start.3 = (f32[1024,256]{0,1:T(8,128)}, f32[1024,256]{0,1:T(8,128)}, u32[]{:S(2)}, u32[]{:S(2)}) collective-permute-start(f32[1024,256]{0,1:T(8,128)} %slice.43), channel_id=1, source_target_pairs={{8,0},{16,8},{24,16},{32,24},{40,32},{48,40},{56,48},{64,56},{72,6... | collective-permute-start | bytes 3145736 | tf_op jit(solution)/shard_map/ppermute | solution.py:16
  167.6 16.9 %all-to-all-start.2 = ((bf16[8,128,256]{2,1,0:T(8,128)(2,1)}), bf16[8,128,256]{2,1,0:T(8,128)(2,1)S(1)}, u32[]{:S(2)}, u32[]{:S(2)}) async-start(bf16[8,128,256]{2,1,0:T(8,128)(2,1)} %bitcast.29), calls=%async_computation.2 | async-start | bytes 1048576 | tf_op jit(solution)/shard_map/all_to_all | solution.py:121
  184.5 13.6 %all-to-all-start.3 = ((bf16[8,128,256]{2,1,0:T(8,128)(2,1)}), bf16[8,128,256]{2,1,0:T(8,128)(2,1)S(1)}, u32[]{:S(2)}, u32[]{:S(2)}) async-start(bf16[8,128,256]{2,1,0:T(8,128)(2,1)} %bitcast.32), calls=%async_computation.3 | async-start | bytes 1048576 | tf_op jit(solution)/shard_map/all_to_all | solution.py:122
where the time goes:
time: 201 us; the launch traced here: 199 us
  matrix products  54.5 us (27%)
  local copies, waits for them, and re-layouts  50.6 us (25%)
  waiting for transfers between devices  47.3 us (24%)
  starting transfers between devices  29.3 us (15%)
  other arithmetic  16.5 us (8%)
    ppermute x4, waiting for transfers between devices, from_behind(): return lax.ppermute(shard, axis, pairs)  28.6 us
    dot_general x2, matrix products, band_tile(): jnp.einsum('qhgd,khd->hgqk', grad_split, value_split, preferred_element_t...  19 us
    dot_general x2, matrix products, band_tile(): jnp.einsum('hgqk,qhgd->khd', probs_low, grad_split, preferred_element_typ...  14 us
    dot_general x2, matrix products, band_tile(): jnp.einsum('qhgd,khd->hgqk', query_split, key_split, preferred_element_ty...  12.7 us
    unnamed x11, local copies, waits for them, and re-layouts  9.99 us
    ppermute x4, starting transfers between devices, from_behind(): return lax.ppermute(shard, axis, pairs)  9.05 us
    all_to_all x1, starting transfers between devices, on_device(): lax.all_to_all(out_grad, 'head', split_axis=1, concat_axis=0, tiled=True)  6.87 us
    all_to_all x1, waiting for transfers between devices, on_device(): lax.all_to_all(own_v, 'head', split_axis=0, concat_axis=1, tiled=True)  6.86 us
  transfers between devices with their start and end apart: 8, of which 6 were waited for; matrix products, arithmetic and copies ran while one was open for 10% of the time, Pallas kernels for 0%

commit v1 on v0

v1 whole, which is shorter than its diff:
```python
import jax
import jax.numpy as jnp
from jax import lax
from jax.experimental import pallas as pl
from jax.experimental.pallas import tpu as pltpu
from jax.sharding import PartitionSpec as P

HEAD_DIM = 128
WINDOW = 1024
TOK = 1024
TILE = 256
PAIR = 2 * HEAD_DIM
SCALE = 168.0**-0.5
LOG2E = 1.4426950408889634
BIG = 1e30

ROWS_ROWS = (((1,), (1,)), ((), ()))
ROWS_COLS = (((1,), (0,)), ((), ()))
COLS_COLS = (((0,), (0,)), ((), ()))


def dot(a, b, dims):
    return lax.dot_general(a, b, dims, preferred_element_type=jnp.float32)


def band_kernel(
    edge_ref, q_ref, o_ref, g_ref, norm_ref, k_rim_ref, v_rim_ref, k_own_ref, v_own_ref,
    dq_ref, rim_ref, own_ref, keys, values, dk_sum, dv_sum, dq_sum, norm, delta,
):
    pair = pl.program_id(0)
    steps = TOK // TILE
    keys[0:TOK] = k_rim_ref[...]
    keys[TOK:] = k_own_ref[...]
    values[0:TOK] = v_rim_ref[...]
    values[TOK:] = v_own_ref[...]
    dk_sum[...] = jnp.zeros_like(dk_sum)
    dv_sum[...] = jnp.zeros_like(dv_sum)
    ones = jnp.ones((8, HEAD_DIM), jnp.bfloat16)
    for h in range(2):
        cols = slice(h * HEAD_DIM, (h + 1) * HEAD_DIM)
        terms = g_ref[:, cols].astype(jnp.float32) * o_ref[:, cols].astype(jnp.float32)
        high = terms.astype(jnp.bfloat16)
        low = (terms - high.astype(jnp.float32)).astype(jnp.bfloat16)
        delta[h] = dot(ones, high, ROWS_ROWS) + dot(ones, low, ROWS_ROWS)
        norm[h] = jnp.broadcast_to(norm_ref[pl.ds(pair * 2 + h, 1), :] * LOG2E, (8, TOK))
    rim_off = edge_ref[0]

    def tile(i, e, kind):
        at_q = pl.ds(pl.multiple_of(i * TILE, TILE), TILE)
        at_k = pl.ds(pl.multiple_of(e * TILE, TILE), TILE)
        k = keys[at_k, :]
        v = values[at_k, :]
        off = jnp.where(e * TILE < TOK, rim_off, 0.0)
        if kind:
            row = lax.broadcasted_iota(jnp.int32, (TILE, TILE), 0)
            col = lax.broadcasted_iota(jnp.int32, (TILE, TILE), 1)
            allowed = row > col if kind == 1 else row <= col
        probs = []
        grads = []
        for h in range(2):
            cols = slice(h * HEAD_DIM, (h + 1) * HEAD_DIM)
            scores = dot(k, q_ref[at_q, cols], ROWS_ROWS)
            prob = jnp.exp2(scores * (SCALE * LOG2E) - (norm[h, 0:1, at_q] + off))
            if kind:
                prob = jnp.where(allowed, prob, 0.0)
            grad_prob = dot(v, g_ref[at_q, cols], ROWS_ROWS)
            grads.append((prob * (grad_prob - delta[h, 0:1, at_q])).astype(jnp.bfloat16))
            probs.append(prob.astype(jnp.bfloat16))
        first, second = slice(0, HEAD_DIM), slice(HEAD_DIM, PAIR)
        dv_sum[at_k, :] += dot(probs[0], g_ref[at_q, first], ROWS_COLS) + dot(
            probs[1], g_ref[at_q, second], ROWS_COLS
        )
        dk_sum[at_k, :] += dot(grads[0], q_ref[at_q, first], ROWS_COLS) + dot(
            grads[1], q_ref[at_q, second], ROWS_COLS
        )
        for h in range(2):
            dq_sum[h] += dot(k, grads[h], COLS_COLS)

    def query_tile(i, carried):
        dq_sum[...] = jnp.zeros_like(dq_sum)
        tile(i, i, 1)
        for a in range(1, steps):
            tile(i, i + a, 0)
        tile(i, i + steps, 2)
        at_q = pl.ds(pl.multiple_of(i * TILE, TILE), TILE)
        for h in range(2):
            cols = slice(h * HEAD_DIM, (h + 1) * HEAD_DIM)
            dq_ref[at_q, cols] = (dq_sum[h] * SCALE).T.astype(jnp.bfloat16)
        return carried

    lax.fori_loop(0, steps, query_tile, 0)
    rim_ref[:, 0:HEAD_DIM] = (dk_sum[0:TOK] * SCALE).astype(jnp.bfloat16)
    rim_ref[:, HEAD_DIM:] = dv_sum[0:TOK].astype(jnp.bfloat16)
    own_ref[:, 0:HEAD_DIM] = dk_sum[TOK:] * SCALE
    own_ref[:, HEAD_DIM:] = dv_sum[TOK:]


def band(edge, q, o, g, norm, k_rim, v_rim, k_own, v_own):
    wide = pl.BlockSpec((TOK, PAIR), lambda i: (0, i))
    narrow = pl.BlockSpec((TOK, HEAD_DIM), lambda i: (0, i))
    shape = jax.ShapeDtypeStruct
    return pl.pallas_call(
        band_kernel,
        grid=(2,),
        in_specs=[
            pl.BlockSpec(memory_space=pltpu.SMEM), wide, wide, wide,
            pl.BlockSpec((4, TOK), lambda i: (0, 0)), narrow, narrow, narrow, narrow,
        ],
        out_specs=[wide, wide, wide],
        out_shape=[
            shape((TOK, 2 * PAIR), jnp.bfloat16),
            shape((TOK, 2 * PAIR), jnp.bfloat16),
            shape((TOK, 2 * PAIR), jnp.float32),
        ],
        scratch_shapes=[
            pltpu.VMEM((2 * TOK, HEAD_DIM), jnp.bfloat16),
            pltpu.VMEM((2 * TOK, HEAD_DIM), jnp.bfloat16),
            pltpu.VMEM((2 * TOK, HEAD_DIM), jnp.float32),
            pltpu.VMEM((2 * TOK, HEAD_DIM), jnp.float32),
            pltpu.VMEM((2, HEAD_DIM, TILE), jnp.float32),
            pltpu.VMEM((2, 8, TOK), jnp.float32),
            pltpu.VMEM((2, 8, TOK), jnp.float32),
        ],
        compiler_params=pltpu.CompilerParams(vmem_limit_bytes=40 * 1024 * 1024),
        cost_estimate=pl.CostEstimate(
            flops=8 * 10**9, bytes_accessed=10 * 2**20, transcendentals=5 * 10**6
        ),
    )(edge, q, o, g, norm, k_rim, v_rim, k_own, v_own)


def from_behind(shard, by):
    devices = lax.axis_size("seq")
    pairs = [(i, i + by) for i in range(devices) if 0 <= i + by < devices]
    return lax.ppermute(shard, "seq", pairs)


def to_heads(x):
    members = lax.axis_size("head")
    rows, width = x.shape
    parts = x.reshape(rows, members, width // members).transpose(1, 0, 2)
    parts = lax.all_to_all(parts, "head", split_axis=0, concat_axis=0, tiled=True)
    return parts.reshape(members * rows, width // members)


def to_tokens(x):
    members = lax.axis_size("head")
    parts = x.reshape(members, x.shape[0] // members, x.shape[1])
    return lax.all_to_all(parts, "head", split_axis=0, concat_axis=0, tiled=True)


def on_device(queries, key_states, value_states, outputs, out_grad, log_norm):
    k_rim = from_behind(key_states, 1)
    v_rim = from_behind(value_states, 1)
    grad_local = to_heads(out_grad)
    edge = jnp.where(lax.axis_index("seq") == 0, BIG, 0.0).astype(jnp.float32).reshape(1)
    dq, rim, own = band(
        edge, queries, outputs, grad_local, log_norm, k_rim, v_rim, key_states, value_states
    )
    later = from_behind(rim, -1)
    dkv = (own + later.astype(jnp.float32)).astype(jnp.bfloat16)
    dq = to_tokens(dq)
    dkv = to_tokens(dkv)
    members, rows, width = dq.shape
    dq = dq.transpose(1, 0, 2).reshape(rows, members * width)
    dkv = dkv.reshape(members, rows, 2, 2, HEAD_DIM).transpose(3, 1, 0, 2, 4)
    dkv = dkv.reshape(2, rows, members * PAIR)
    return dq, dkv[0], dkv[1]


def solution(mesh):
    placed = (
        P("seq", "head"),
        P("seq", "head"),
        P("seq", "head"),
        P("seq", "head"),
        P(("seq", "head"), None),
        P("head", "seq"),
    )
    return jax.shard_map(
        on_device,
        mesh=mesh,
        in_specs=placed,
        out_specs=(P(("seq", "head"), None), P(("seq", "head"), None), P(("seq", "head"), None)),
        check_vma=False,
    )
```

time: 201 us -> 117 us (0.58)
  matrix products: 54.5 us -> 0 us
  local copies, waits for them, and re-layouts: 50.6 us -> 16.6 us
  Pallas kernels: 0 us -> 19.8 us
  other arithmetic: 16.5 us -> 2.54 us
  waiting for transfers between devices: 47.3 us -> 52.5 us
  starting transfers between devices: 29.3 us -> 24.2 us
    dot_general x10 -> x0, matrix products: 54.5 us -> none  [the longest x2 19 us: band_tile(): jnp.einsum('qhgd,khd->hgqk', grad_split, value_split, preferred_element_t...]
    pallas_call x0 -> x1, Pallas kernels: none -> 19.8 us  [band(): pl.pallas_call(band_kernel, grid=(2,), in_specs=[pl.BlockSpec(memory_spac...]
    dynamic_slice x16 -> x0, local copies, waits for them, and re-layouts: 16.4 us -> none  [the longest x4 6.25 us: one_block(): q_rows = lax.dynamic_slice_in_dim(queries, row_start, block_rows, 0)]
    unnamed x2 -> x0, other arithmetic: 4.35 us -> none
    concatenate x2 -> x0, other arithmetic: 4.23 us -> none  [the longest x1 2.12 us: on_device(): key_ext = jnp.concatenate([key_rim, key_states], 0)]
    dynamic_update_slice x4 -> x0, local copies, waits for them, and re-layouts: 4.17 us -> none  [one_block(): lax.dynamic_update_slice_in_dim(grad_q_all, grad_q.astype(jnp.bfloat16),...]
    all_to_all x5 -> x0, local copies, waits for them, and re-layouts: 4.17 us -> none  [the longest x2 2.97 us: on_device(): lax.all_to_all(out_grad, 'head', split_axis=1, concat_axis=0, tiled=True)]
    ppermute x4 -> x3, waiting for transfers between devices: 28.6 us -> 32.2 us  [from_behind(): return lax.ppermute(shard, 'seq', pairs)]
  transfers between devices with their start and end apart: 8 -> 6, of which waited for: 6 -> 5; matrix products, arithmetic and copies ran while one was open for 10% -> 3% of each run, Pallas kernels for 0% -> 0%
where the time goes in v1:
time: 117 us; the launch traced here: 116 us
  waiting for transfers between devices  52.5 us (45%)
  starting transfers between devices  24.2 us (21%)
  Pallas kernels  19.8 us (17%)
  local copies, waits for them, and re-layouts  16.6 us (14%)
  other arithmetic  2.54 us (2%)
    ppermute x3, waiting for transfers between devices, from_behind(): return lax.ppermute(shard, 'seq', pairs)  32.2 us
    all_to_all x2, waiting for transfers between devices, to_tokens(): lax.all_to_all(parts, 'head', split_axis=0, concat_axis=0, tiled=True)  20.3 us
    pallas_call x1, Pallas kernels, band(): pl.pallas_call(band_kernel, grid=(2,), in_specs=[pl.BlockSpec(memory_spac...  19.8 us
    all_to_all x2, starting transfers between devices, to_tokens(): lax.all_to_all(parts, 'head', split_axis=0, concat_axis=0, tiled=True)  9.89 us
    unnamed x24, local copies, waits for them, and re-layouts  9.22 us
    ppermute x3, starting transfers between devices, from_behind(): return lax.ppermute(shard, 'seq', pairs)  7.42 us
    all_to_all x1, starting transfers between devices, to_heads(): lax.all_to_all(parts, 'head', split_axis=0, concat_axis=0, tiled=True)  6.87 us
    convert_element_type x1, other arithmetic, on_device(): dkv = (own + later.astype(jnp.float32)).astype(jnp.bfloat16)  2.54 us
  transfers between devices with their start and end apart: 6, of which 5 were waited for; matrix products, arithmetic and copies ran while one was open for 3% of the time, Pallas kernels for 0%

profile of v1, /device:TPU:2, one launch (start us, length us, event | category | flops | bytes accessed | tf_op | source)
XLA Modules:
  0.0 116.4 jit_solution(13755556557513066373)
XLA Ops:
  0.6 0.0 copy-start.3
  0.6 0.0 copy-start.5
  0.7 0.0 copy-start.11
  0.7 2.4 %copy.16 = bf16[16,8,8,512]{3,2,0,1:T(8,128)(2,1)} copy(bf16[16,8,8,512]{3,2,1,0:T(8,128)(2,1)} %bitcast.22) | data formatting | bytes 2097152 | tf_op jit(solution)/shard_map/reshape | solution.py:140
  3.0 6.9 %all-to-all-start = ((bf16[8,128,512]{2,1,0:T(8,128)(2,1)}), bf16[8,128,512]{2,1,0:T(8,128)(2,1)S(1)}, u32[]{:S(2)}, u32[]{:S(2)}) async-start(bf16[8,128,512]{2,1,0:T(8,128)(2,1)} %bitcast.15), calls=%async_computation | async-start | bytes 2097152 | tf_op jit(solution)/shard_map/all_to_all | solution.py:141
  9.9 0.0 copy-done.3
  9.9 1.9 %collective-permute-start = (bf16[1024,256]{1,0:T(8,128)(2,1)S(1)}, bf16[1024,256]{1,0:T(8,128)(2,1)S(1)}, u32[]{:S(2)}, u32[]{:S(2)}) collective-permute-start(bf16[1024,256]{1,0:T(8,128)(2,1)S(1)} %copy-done.3), channel_id=1, source_target_pairs={{0,8},{8,16},{16,24},{24,32},{32,40},{40,48},{48,56},{56,64},{64,7... | collective-permute-start | bytes 1572872 | tf_op jit(solution)/shard_map/ppermute | solution.py:134
  11.9 0.0 copy-done.5
  11.9 3.6 %collective-permute-start.1 = (bf16[1024,256]{1,0:T(8,128)(2,1)S(1)}, bf16[1024,256]{1,0:T(8,128)(2,1)S(1)}, u32[]{:S(2)}, u32[]{:S(2)}) collective-permute-start(bf16[1024,256]{1,0:T(8,128)(2,1)S(1)} %copy-done.5), channel_id=1, source_target_pairs={{0,8},{8,16},{16,24},{24,32},{32,40},{40,48},{48,56},{56,64},{64,7... | collective-permute-start | bytes 1572872 | tf_op jit(solution)/shard_map/ppermute | solution.py:134
  15.5 15.8 %collective-permute-done.k_rim_ref = bf16[1024,256]{1,0:T(8,128)(2,1)S(1)} collective-permute-done((bf16[1024,256]{1,0:T(8,128)(2,1)S(1)}, bf16[1024,256]{1,0:T(8,128)(2,1)S(1)}, u32[]{:S(2)}, u32[]{:S(2)}) %collective-permute-start) | collective-permute-done | bytes 524320 | tf_op jit(solution)/shard_map/ppermute | solution.py:134
  31.3 0.0 copy-start.7
  31.3 0.8 copy-done.7
  32.1 4.8 %collective-permute-done.1.v_rim_ref = bf16[1024,256]{1,0:T(8,128)(2,1)S(1)} collective-permute-done((bf16[1024,256]{1,0:T(8,128)(2,1)S(1)}, bf16[1024,256]{1,0:T(8,128)(2,1)S(1)}, u32[]{:S(2)}, u32[]{:S(2)}) %collective-permute-start.1) | collective-permute-done | bytes 524320 | tf_op jit(solution)/shard_map/ppermute | solution.py:134
  36.9 0.0 copy-start.9
  36.9 0.8 copy-done.9
  37.7 0.0 all-to-all-done
  37.7 0.0 copy-done.11
  37.7 0.0 copy-start.1
  37.7 1.2 %copy-done.1 = bf16[1024,512]{1,0:T(8,128)(2,1)S(1)} copy-done((bf16[1024,512]{1,0:T(8,128)(2,1)S(1)}, bf16[1024,512]{1,0:T(8,128)(2,1)}, u32[]{:S(2)}) %copy-start.1) | copy-done | bytes 1048600
  38.9 0.0 copy-start.2
  38.9 1.2 %copy-done.2 = bf16[1024,512]{1,0:T(8,128)(2,1)S(1)} copy-done((bf16[1024,512]{1,0:T(8,128)(2,1)S(1)}, bf16[1024,512]{1,0:T(8,128)(2,1)}, u32[]{:S(2)}) %copy-start.2) | copy-done | bytes 1048600
  40.1 0.0 copy-start.4
  40.1 1.0 copy-done.4
  41.2 0.0 copy-start.6
  41.2 1.0 copy-done.6
  42.2 0.0 copy-start.8
  42.2 1.0 copy-done.8
  43.3 0.0 copy-start.10
  43.3 1.0 copy-done.10
  44.3 19.8 %shard_map.85 = (bf16[1024,512]{1,0:T(8,128)(2,1)S(1)}, bf16[1024,512]{1,0:T(8,128)(2,1)}, f32[1024,512]{1,0:T(8,128)S(1)}) custom-call(f32[1]{0:T(128)} %bitcast.edge_ref, bf16[1024,512]{1,0:T(8,128)(2,1)S(1)} %copy-done.1, bf16[1024,512]{1,0:T(8,128)(2,1)S(1)} %copy-done.2, bf16[1024,512]{1,0:T(8,128)(2,1)S(1)} %bitcast.17, f32[4,1024]{1,0:T(4,128)S(1)} %copy-done.11, ...), custom_call_target="tpu_custom_call" | custom-call | flops 8000000000 | bytes 10485760 | tf_op jit(solution)/shard_map/pallas_call | solution.py:102
  64.1 0.0 copy-start
  64.1 1.0 copy-done
  65.1 1.9 %collective-permute-start.2 = (bf16[1024,512]{1,0:T(8,128)(2,1)}, bf16[1024,512]{1,0:T(8,128)(2,1)}, u32[]{:S(2)}, u32[]{:S(2)}) collective-permute-start(bf16[1024,512]{1,0:T(8,128)(2,1)} %get-tuple-element.8), channel_id=1, source_target_pairs={{8,0},{16,8},{24,16},{32,24},{40,32},{48,40},{56,48},{64,56},{72,6... | collective-permute-start | bytes 3145736 | tf_op jit(solution)/shard_map/ppermute | solution.py:134
  67.0 6.3 %all-to-all-start.1 = ((bf16[8,128,512]{2,1,0:T(8,128)(2,1)}), bf16[8,128,512]{2,1,0:T(8,128)(2,1)S(1)}, u32[]{:S(2)}, u32[]{:S(2)}) async-start(bf16[8,128,512]{2,1,0:T(8,128)(2,1)} %bitcast.18), calls=%async_computation.1 | async-start | bytes 2097152 | tf_op jit(solution)/shard_map/all_to_all | solution.py:148
  73.3 11.6 %collective-permute-done.2 = bf16[1024,512]{1,0:T(8,128)(2,1)} collective-permute-done((bf16[1024,512]{1,0:T(8,128)(2,1)}, bf16[1024,512]{1,0:T(8,128)(2,1)}, u32[]{:S(2)}, u32[]{:S(2)}) %collective-permute-start.2) | collective-permute-done | bytes 1048608 | tf_op jit(solution)/shard_map/ppermute | solution.py:134
  85.0 2.5 %add_convert_fusion = bf16[1024,512]{1,0:T(8,128)(2,1)} fusion(f32[1024,512]{1,0:T(8,128)S(1)} %get-tuple-element.7, bf16[1024,512]{1,0:T(8,128)(2,1)} %collective-permute-done.2), kind=kLoop, calls=%fused_computation | loop fusion | flops 1572864 | bytes 4194304 | tf_op jit(solution)/shard_map/convert_element_type | solution.py:160
  87.5 8.4 %all-to-all-done.1 = bf16[8,128,512]{2,1,0:T(8,128)(2,1)S(1)} async-done(((bf16[8,128,512]{2,1,0:T(8,128)(2,1)}), bf16[8,128,512]{2,1,0:T(8,128)(2,1)S(1)}, u32[]{:S(2)}, u32[]{:S(2)}) %all-to-all-start.1) | async-done | bytes 1048608 | tf_op jit(solution)/shard_map/all_to_all | solution.py:148
  95.9 3.6 %all-to-all-start.2 = ((bf16[8,128,512]{2,1,0:T(8,128)(2,1)}), bf16[8,128,512]{2,1,0:T(8,128)(2,1)S(1)}, u32[]{:S(2)}, u32[]{:S(2)}) async-start(bf16[8,128,512]{2,1,0:T(8,128)(2,1)} %bitcast.21), calls=%async_computation.2 | async-start | bytes 2097152 | tf_op jit(solution)/shard_map/all_to_all | solution.py:148
  99.5 1.1 copy.13
  100.6 11.9 %all-to-all-done.2 = bf16[8,128,512]{2,1,0:T(8,128)(2,1)S(1)} async-done(((bf16[8,128,512]{2,1,0:T(8,128)(2,1)}), bf16[8,128,512]{2,1,0:T(8,128)(2,1)S(1)}, u32[]{:S(2)}, u32[]{:S(2)}) %all-to-all-start.2) | async-done | bytes 1048608 | tf_op jit(solution)/shard_map/all_to_all | solution.py:148
  112.4 0.3 reshape.38
  112.7 0.5 copy.17
  113.3 0.7 fusion
  114.0 1.2 %squeeze.7 = bf16[128,2048]{1,0:T(8,128)(2,1)} reshape(bf16[1,128,8,2,128]{4,3,2,1,0:T(2,128)(2,1)S(1)} %get-tuple-element.9) | data formatting | bytes 1048576 | tf_op jit(solution)/shard_map/squeeze | solution.py:167
  115.2 1.2 %squeeze.6 = bf16[128,2048]{1,0:T(8,128)(2,1)} reshape(bf16[1,128,8,2,128]{4,3,2,1,0:T(2,128)(2,1)S(1)} %get-tuple-element.10) | data formatting | bytes 1048576 | tf_op jit(solution)/shard_map/squeeze | solution.py:167
Async XLA Ops:
  0.6 9.3 %copy-start.3 = (bf16[1024,256]{1,0:T(8,128)(2,1)S(1)}, bf16[1024,256]{1,0:T(8,128)(2,1)}, u32[]{:S(2)}) copy-start(bf16[1024,256]{1,0:T(8,128)(2,1)} %k_own_ref.1) | copy-start | bytes 1572868
  0.6 11.2 %copy-start.5 = (bf16[1024,256]{1,0:T(8,128)(2,1)S(1)}, bf16[1024,256]{1,0:T(8,128)(2,1)}, u32[]{:S(2)}) copy-start(bf16[1024,256]{1,0:T(8,128)(2,1)} %v_own_ref.1) | copy-start | bytes 1572868
  0.7 37.0 %copy-start.11 = (f32[4,1024]{1,0:T(4,128)S(1)}, f32[4,1024]{1,0:T(4,128)}, u32[]{:S(2)}) copy-start(f32[4,1024]{1,0:T(4,128)} %norm_ref.1) | copy-start | bytes 49156
  3.0 34.6 %all-to-all-start = ((bf16[8,128,512]{2,1,0:T(8,128)(2,1)}), bf16[8,128,512]{2,1,0:T(8,128)(2,1)S(1)}, u32[]{:S(2)}, u32[]{:S(2)}) async-start(bf16[8,128,512]{2,1,0:T(8,128)(2,1)} %bitcast.15), calls=%async_computation | async-start | bytes 2097152 | tf_op jit(solution)/shard_map/all_to_all | solution.py:141
  9.9 21.3 %collective-permute-start = (bf16[1024,256]{1,0:T(8,128)(2,1)S(1)}, bf16[1024,256]{1,0:T(8,128)(2,1)S(1)}, u32[]{:S(2)}, u32[]{:S(2)}) collective-permute-start(bf16[1024,256]{1,0:T(8,128)(2,1)S(1)} %copy-done.3), channel_id=1, source_target_pairs={{0,8},{8,16},{16,24},{24,32},{32,40},{40,48},{48,56},{56,64},{64,7... | collective-permute-start | bytes 1572872 | tf_op jit(solution)/shard_map/ppermute | solution.py:134
  11.9 25.0 %collective-permute-start.1 = (bf16[1024,256]{1,0:T(8,128)(2,1)S(1)}, bf16[1024,256]{1,0:T(8,128)(2,1)S(1)}, u32[]{:S(2)}, u32[]{:S(2)}) collective-permute-start(bf16[1024,256]{1,0:T(8,128)(2,1)S(1)} %copy-done.5), channel_id=1, source_target_pairs={{0,8},{8,16},{16,24},{24,32},{32,40},{40,48},{48,56},{56,64},{64,7... | collective-permute-start | bytes 1572872 | tf_op jit(solution)/shard_map/ppermute | solution.py:134
  31.3 0.8 copy-start.7
  36.9 0.8 copy-start.9
  37.7 1.2 %copy-start.1 = (bf16[1024,512]{1,0:T(8,128)(2,1)S(1)}, bf16[1024,512]{1,0:T(8,128)(2,1)}, u32[]{:S(2)}) copy-start(bf16[1024,512]{1,0:T(8,128)(2,1)} %q_ref.1) | copy-start | bytes 3145732
  38.9 1.2 %copy-start.2 = (bf16[1024,512]{1,0:T(8,128)(2,1)S(1)}, bf16[1024,512]{1,0:T(8,128)(2,1)}, u32[]{:S(2)}) copy-start(bf16[1024,512]{1,0:T(8,128)(2,1)} %o_ref.1) | copy-start | bytes 3145732
  40.1 1.0 copy-start.4
  41.2 1.0 copy-start.6
  42.2 1.0 copy-start.8
  43.3 1.0 copy-start.10
  64.1 1.0 copy-start
  65.1 19.9 %collective-permute-start.2 = (bf16[1024,512]{1,0:T(8,128)(2,1)}, bf16[1024,512]{1,0:T(8,128)(2,1)}, u32[]{:S(2)}, u32[]{:S(2)}) collective-permute-start(bf16[1024,512]{1,0:T(8,128)(2,1)} %get-tuple-element.8), channel_id=1, source_target_pairs={{8,0},{16,8},{24,16},{32,24},{40,32},{48,40},{56,48},{64,56},{72,6... | collective-permute-start | bytes 3145736 | tf_op jit(solution)/shard_map/ppermute | solution.py:134
  67.0 28.9 %all-to-all-start.1 = ((bf16[8,128,512]{2,1,0:T(8,128)(2,1)}), bf16[8,128,512]{2,1,0:T(8,128)(2,1)S(1)}, u32[]{:S(2)}, u32[]{:S(2)}) async-start(bf16[8,128,512]{2,1,0:T(8,128)(2,1)} %bitcast.18), calls=%async_computation.1 | async-start | bytes 2097152 | tf_op jit(solution)/shard_map/all_to_all | solution.py:148
  95.9 16.5 %all-to-all-start.2 = ((bf16[8,128,512]{2,1,0:T(8,128)(2,1)}), bf16[8,128,512]{2,1,0:T(8,128)(2,1)S(1)}, u32[]{:S(2)}, u32[]{:S(2)}) async-start(bf16[8,128,512]{2,1,0:T(8,128)(2,1)} %bitcast.21), calls=%async_computation.2 | async-start | bytes 2097152 | tf_op jit(solution)/shard_map/all_to_all | solution.py:148

commit v2 on v1

v2 whole, which is shorter than its diff:
```python
import functools

import jax
import jax.numpy as jnp
from jax import lax
from jax.experimental import pallas as pl
from jax.experimental.pallas import tpu as pltpu
from jax.sharding import PartitionSpec as P


HEAD_DIM = 128
TOK = 1024
TILE = 256
PAIR = 2 * HEAD_DIM
SCALE = 168.0**-0.5
LOG2E = 1.4426950408889634
BIG = 1e30

ROWS_ROWS = (((1,), (1,)), ((), ()))
ROWS_COLS = (((1,), (0,)), ((), ()))
COLS_COLS = (((0,), (0,)), ((), ()))


def dot(a, b, dims):
    return lax.dot_general(a, b, dims, preferred_element_type=jnp.float32)


HEADS = [slice(h * HEAD_DIM, (h + 1) * HEAD_DIM) for h in range(2)]
STEPS = TOK // TILE


def band_kernel(own, *refs):
    if own:
        norm_ref, q_ref, g_ref, delta_ref, k_ref, v_ref, part_ref, dq_ref, dkv_ref = refs[:9]
    else:
        edge_ref, norm_ref, *refs = refs
        q_ref, g_ref, o_ref, k_ref, va_ref, *vb_refs = refs[:7]
        part_ref, dkv_ref, delta_ref, v_ref = refs[7:11]
    norm, dk_sum, dv_sum = refs[-3:]
    pair = pl.program_id(0)
    for h in range(2):
        row = norm_ref[pl.ds(pair * 2 + h, 1), :] * LOG2E
        if not own:
            row = row + edge_ref[0]
        norm[h] = jnp.broadcast_to(row, (8, TOK))

    if not own:
        for n, vb_ref in enumerate(vb_refs):
            at = slice(n * TOK // 2, (n + 1) * TOK // 2)
            v_ref[at, :] = va_ref[at, :] + vb_ref[...]
        ones = jnp.ones((8, HEAD_DIM), jnp.bfloat16)
        for h in range(2):
            terms = g_ref[:, HEADS[h]].astype(jnp.float32) * o_ref[:, HEADS[h]].astype(jnp.float32)
            high = terms.astype(jnp.bfloat16)
            low = (terms - high.astype(jnp.float32)).astype(jnp.bfloat16)
            total = dot(ones, high, ROWS_ROWS) + dot(ones, low, ROWS_ROWS)
            delta_ref[8 * h : 8 * h + 8, :] = total

    def tile(i, e, dq):
        at_q = slice(i * TILE, (i + 1) * TILE)
        at_k = slice(e * TILE, (e + 1) * TILE)
        k = k_ref[at_k, :]
        v = v_ref[at_k, :]
        if i == e:
            row = lax.broadcasted_iota(jnp.int32, (TILE, TILE), 0)
            col = lax.broadcasted_iota(jnp.int32, (TILE, TILE), 1)
            allowed = row <= col if own else row > col
        probs = []
        grads = []
        for h in range(2):
            scores = dot(k, q_ref[at_q, HEADS[h]], ROWS_ROWS)
            prob = jnp.exp2(scores * (SCALE * LOG2E) - norm[h, 0:1, at_q])
            if i == e:
                prob = jnp.where(allowed, prob, 0.0)
            grad_prob = dot(v, g_ref[at_q, HEADS[h]], ROWS_ROWS)
            delta = delta_ref[8 * h : 8 * h + 1, at_q]
            grads.append((prob * (grad_prob - delta)).astype(jnp.bfloat16))
            probs.append(prob.astype(jnp.bfloat16))
        dv = dot(probs[0], g_ref[at_q, HEADS[0]], ROWS_COLS) + dot(
            probs[1], g_ref[at_q, HEADS[1]], ROWS_COLS
        )
        dk = dot(grads[0], q_ref[at_q, HEADS[0]], ROWS_COLS) + dot(
            grads[1], q_ref[at_q, HEADS[1]], ROWS_COLS
        )
        if i == (e if own else 0):
            dv_sum[at_k, :] = dv
            dk_sum[at_k, :] = dk
        else:
            dv_sum[at_k, :] += dv
            dk_sum[at_k, :] += dk
        return [d + dot(k, grads[h], COLS_COLS) for h, d in enumerate(dq)]

    for i in range(STEPS):
        at_q = slice(i * TILE, (i + 1) * TILE)
        if own:
            dq = [part_ref[rows, at_q] for rows in HEADS]
        else:
            dq = [jnp.zeros((HEAD_DIM, TILE), jnp.float32)] * 2
        for e in range(0, i + 1) if own else range(i, STEPS):
            dq = tile(i, e, dq)
        for h in range(2):
            if own:
                dq_ref[at_q, HEADS[h]] = (dq[h] * SCALE).T.astype(jnp.bfloat16)
            else:
                part_ref[HEADS[h], at_q] = dq[h]
    kind = dkv_ref.dtype
    dkv_ref[:, 0:HEAD_DIM] = (dk_sum[...] * SCALE).astype(kind)
    dkv_ref[:, HEAD_DIM:] = dv_sum[...].astype(kind)


def band(own, *operands):
    spec = pl.BlockSpec
    wide = spec((TOK, PAIR), lambda i: (0, i))
    tall = spec((PAIR, TOK), lambda i: (i, 0))
    narrow = spec((TOK, HEAD_DIM), lambda i: (0, i))
    lines = spec((16, TOK), lambda i: (i, 0))
    shape = jax.ShapeDtypeStruct
    norm = spec((4, TOK), lambda i: (0, 0))
    scratch = [
        pltpu.VMEM((2, 8, TOK), jnp.float32),
        pltpu.VMEM((TOK, HEAD_DIM), jnp.float32),
        pltpu.VMEM((TOK, HEAD_DIM), jnp.float32),
    ]
    if own:
        in_specs = [norm, wide, wide, lines, narrow, narrow, tall]
        out_specs = [wide, wide]
        out_shape = [
            pltpu.HBM((TOK, 2 * PAIR), jnp.bfloat16),
            shape((TOK, 2 * PAIR), jnp.float32),
        ]
    else:
        half = spec((TOK // 2, HEAD_DIM), lambda i: (0, i))
        in_specs = [spec(memory_space=pltpu.SMEM), norm, wide, wide, wide, narrow, narrow, half, half]
        out_specs = [tall, wide, lines]
        out_shape = [
            shape((2 * PAIR, TOK), jnp.float32),
            shape((TOK, 2 * PAIR), jnp.bfloat16),
            shape((32, TOK), jnp.float32),
        ]
        scratch = [pltpu.VMEM((TOK, HEAD_DIM), jnp.bfloat16)] + scratch
    return pl.pallas_call(
        functools.partial(band_kernel, own),
        name="own_band" if own else "rim_band",
        grid=(2,),
        in_specs=in_specs,
        out_specs=out_specs,
        out_shape=out_shape,
        scratch_shapes=scratch,
        compiler_params=pltpu.CompilerParams(vmem_limit_bytes=24000 * 1024),
        cost_estimate=pl.CostEstimate(
            flops=4 * 10**9, bytes_accessed=8 * 2**20, transcendentals=3 * 10**6
        ),
    )(*operands)


def from_behind(shard, by, skip=None):
    devices = lax.axis_size("seq")
    pairs = [(i, i + by) for i in range(devices) if 0 <= i + by < devices and i != skip]
    return lax.ppermute(shard, "seq", pairs)


def prepare_kernel(g_ref, parts_ref, sem):
    members, _, width = parts_ref.shape
    copies = [
        pltpu.make_async_copy(g_ref.at[:, pl.ds(i * width, width)], parts_ref.at[i], sem.at[i])
        for i in range(members)
    ]
    for copy in copies:
        copy.start()
    for copy in copies:
        copy.wait()


def prepare(out_grad):
    members = lax.axis_size("head")
    rows, width = out_grad.shape
    shape = (members, rows, width // members)
    return pl.pallas_call(
        prepare_kernel,
        name="prepare",
        grid=(1,),
        in_specs=[pl.BlockSpec(memory_space=pl.ANY)],
        out_specs=pl.BlockSpec(shape, lambda i: (0, 0, 0)),
        out_shape=jax.ShapeDtypeStruct(shape, out_grad.dtype),
        scratch_shapes=[pltpu.SemaphoreType.DMA((members,))],
        compiler_params=pltpu.CompilerParams(vmem_limit_bytes=60 * 1024 * 1024),
        cost_estimate=pl.CostEstimate(flops=0, bytes_accessed=2 * 2**20, transcendentals=0),
    )(out_grad)


HOPS = [(0, 0), (1, 0), (0, 1), (3, 0), (2, 1), (2, 0), (1, 1), (3, 1)]


def sum_kernel(me_ref, own_ref, later_ref, *out_refs):
    rows = out_refs[0].shape[0]
    for hop, out_ref in zip(HOPS, out_refs):
        at = pl.ds(pl.multiple_of(partner(me_ref[0], hop) * rows, rows), rows)
        total = own_ref[at, :] + later_ref[at, :].astype(jnp.float32)
        out_ref[...] = total.astype(out_ref.dtype)


def sum_parts(me, own, later):
    members = lax.axis_size("head")
    rows = TOK // members
    vmem = pl.BlockSpec(memory_space=pltpu.VMEM)
    return pl.pallas_call(
        sum_kernel,
        name="sum_parts",
        in_specs=[pl.BlockSpec(memory_space=pltpu.SMEM), vmem, vmem],
        out_specs=[vmem] * members,
        out_shape=[jax.ShapeDtypeStruct((rows, 2 * PAIR), jnp.bfloat16)] * members,
        compiler_params=pltpu.CompilerParams(vmem_limit_bytes=16 * 2**20),
        cost_estimate=pl.CostEstimate(flops=10**6, bytes_accessed=4 * 2**20, transcendentals=0),
    )(me, own, later)


def join_kernel(me_ref, *refs):
    *in_refs, key_ref, value_ref = refs
    for shift, in_ref in enumerate(in_refs):
        source = partner(me_ref[0], (4 - HOPS[shift][0], HOPS[shift][1]))
        for g in range(2):
            to = pl.ds(pl.multiple_of(source * PAIR + g * HEAD_DIM, HEAD_DIM), HEAD_DIM)
            key_ref[:, to] = in_ref[:, g * PAIR : g * PAIR + HEAD_DIM]
            value_ref[:, to] = in_ref[:, g * PAIR + HEAD_DIM : (g + 1) * PAIR]


def join(me, parts):
    members = len(parts)
    rows = parts[0].shape[0]
    vmem = pl.BlockSpec(memory_space=pltpu.VMEM)
    out = jax.ShapeDtypeStruct((rows, members * PAIR), parts[0].dtype)
    return pl.pallas_call(
        join_kernel,
        name="join",
        grid=(1,),
        in_specs=[pl.BlockSpec(memory_space=pltpu.SMEM)]
        + [pl.BlockSpec(parts[0].shape, lambda i: (0, 0))] * members,
        out_specs=[pl.BlockSpec(out.shape, lambda i: (0, 0))] * 2,
        out_shape=[out, out],
        compiler_params=pltpu.CompilerParams(vmem_limit_bytes=16 * 2**20),
        cost_estimate=pl.CostEstimate(flops=0, bytes_accessed=4 * 2**20, transcendentals=0),
    )(me, *parts)


def exchange(parts):
    return lax.all_to_all(parts, "head", split_axis=0, concat_axis=0, tiled=True)


def partner(i, hop):
    z, half = hop
    return (i + 2 * z) % 8 ^ half


def shift_heads(x, hop):
    return lax.ppermute(x, "head", [(i, partner(i, hop)) for i in range(8)])


def on_device(queries, key_states, value_states, outputs, out_grad, log_norm):
    members = lax.axis_size("head")
    me = lax.axis_index("head").astype(jnp.int32).reshape(1)
    edge = jnp.where(lax.axis_index("seq") == 0, BIG, 0.0).astype(jnp.float32).reshape(1)
    half = lax.axis_size("seq") // 2
    middle = (1, half - 3)
    detours = []
    for n in range(2):
        rows = value_states[n * TOK // 2 : (n + 1) * TOK // 2]
        detours.append(lax.ppermute(rows, "seq", [(half - 1, middle[n])]))
    k_rim = from_behind(key_states, 1)
    v_rim = from_behind(value_states, 1, skip=half - 1)
    grad_parts = prepare(out_grad)
    grad_local = exchange(grad_parts).reshape(TOK, 2 * PAIR)
    v_far = []
    for n in range(2):
        v_far.append(lax.ppermute(detours[n], "seq", [(middle[n], half)]))
    queries = pltpu.with_memory_space_constraint(queries, pltpu.HBM)
    part, rim, delta = band(
        False, edge, log_norm, queries, grad_local, outputs, k_rim, v_rim, *v_far
    )
    later = from_behind(rim, -1)
    dq, own = band(True, log_norm, queries, grad_local, delta, key_states, value_states, part)
    dq = exchange(dq.reshape(members, TOK // members, 2 * PAIR))
    dkv = sum_parts(me, own, later)
    dkv = [dkv[0]] + [shift_heads(x, hop) for x, hop in zip(dkv[1:], HOPS[1:])]
    key_grad, value_grad = join(me, dkv)
    dq = dq.transpose(1, 0, 2).reshape(TOK // members, members * 2 * PAIR)
    return dq, key_grad, value_grad


def solution(mesh):
    placed = (
        P("seq", "head"),
        P("seq", "head"),
        P("seq", "head"),
        P("seq", "head"),
        P(("seq", "head"), None),
        P("head", "seq"),
    )
    return jax.shard_map(
        on_device,
        mesh=mesh,
        in_specs=placed,
        out_specs=(P(("seq", "head"), None), P(("seq", "head"), None), P(("seq", "head"), None)),
        check_vma=False,
    )
```

time: 117 us -> 96.3 us (0.82)
  waiting for transfers between devices: 52.5 us -> 23.8 us
  starting transfers between devices: 24.2 us -> 43 us
  local copies, waits for them, and re-layouts: 16.6 us -> 2.38 us
  Pallas kernels: 19.8 us -> 25.3 us
  other arithmetic: 2.54 us -> 0 us
    ppermute x3, waiting for transfers between devices: 32.2 us -> 2.33 us  [from_behind(): return lax.ppermute(shard, 'seq', pairs)]
    ppermute x0 -> x11, waiting for transfers between devices: none -> 21.5 us  [the longest x7 11.4 us: shift_heads(): return lax.ppermute(x, 'head', [(i, partner(i, hop)) for i in range(8)])]
    ppermute x0 -> x11, starting transfers between devices: none -> 21.4 us  [the longest x7 16 us: shift_heads(): return lax.ppermute(x, 'head', [(i, partner(i, hop)) for i in range(8)])]
    all_to_all x3 -> x2, waiting for transfers between devices: 20.3 us -> 0.01 us  [exchange(): lax.all_to_all(parts, 'head', split_axis=0, concat_axis=0, tiled=True)]
    unnamed x24 -> x12, local copies, waits for them, and re-layouts: 9.22 us -> 0.04 us
    pallas_call x1 -> x5, Pallas kernels: 19.8 us -> 25.3 us  [the longest x2 20.2 us: band(): pl.pallas_call(functools.partial(band_kernel, own), name='own_band' if ow...]
    all_to_all x3 -> x2, starting transfers between devices: 16.8 us -> 13.4 us  [exchange(): lax.all_to_all(parts, 'head', split_axis=0, concat_axis=0, tiled=True)]
    convert_element_type x1 -> x0, other arithmetic: 2.54 us -> none  [on_device(): dkv = (own + later.astype(jnp.float32)).astype(jnp.bfloat16)]
  transfers between devices with their start and end apart: 6 -> 16, of which waited for: 5 -> 5; matrix products, arithmetic and copies ran while one was open for 3% -> 2% of each run, Pallas kernels for 0% -> 12%
where the time goes in v2:
time: 96.3 us; the launch traced here: 95.3 us
  starting transfers between devices  43 us (45%)
  Pallas kernels  25.3 us (26%)
  waiting for transfers between devices  23.8 us (25%)
  local copies, waits for them, and re-layouts  2.38 us (2%)
    pallas_call x2, Pallas kernels, band(): pl.pallas_call(functools.partial(band_kernel, own), name='own_band' if ow...  20.2 us
    ppermute x7, starting transfers between devices, shift_heads(): return lax.ppermute(x, 'head', [(i, partner(i, hop)) for i in range(8)])  16 us
    all_to_all x2, starting transfers between devices, exchange(): lax.all_to_all(parts, 'head', split_axis=0, concat_axis=0, tiled=True)  13.4 us
    ppermute x7, waiting for transfers between devices, shift_heads(): return lax.ppermute(x, 'head', [(i, partner(i, hop)) for i in range(8)])  11.4 us
    ppermute x2, waiting for transfers between devices, on_device(): v_far.append(lax.ppermute(detours[n], 'seq', [(middle[n], half)]))  10.1 us
    ppermute x3, starting transfers between devices, from_behind(): return lax.ppermute(shard, 'seq', pairs)  8.23 us
    ppermute x2, starting transfers between devices, on_device(): detours.append(lax.ppermute(rows, 'seq', [(half - 1, middle[n])]))  2.76 us
    ppermute x2, starting transfers between devices, on_device(): v_far.append(lax.ppermute(detours[n], 'seq', [(middle[n], half)]))  2.57 us
  transfers between devices with their start and end apart: 16, of which 5 were waited for; matrix products, arithmetic and copies ran while one was open for 2% of the time, Pallas kernels for 12%

profile of v2, /device:TPU:2, one launch (start us, length us, event | category | flops | bytes accessed | tf_op | source)
XLA Modules:
  0.0 95.3 jit_solution(8759534481740054391)
XLA Ops:
  0.6 0.0 copy-start
  0.6 2.4 %prepare.1 = bf16[8,128,512]{2,1,0:T(8,128)(2,1)} custom-call(bf16[128,4096]{1,0:T(8,128)(2,1)} %g_ref.1), custom_call_target="tpu_custom_call" | custom-call | bytes 2097152 | tf_op jit(solution)/shard_map/prepare/pallas_call | solution.py:178
  3.0 0.0 copy-start.3
  3.0 0.0 copy-start.2
  3.0 0.0 copy-start.5
  3.1 7.0 %all-to-all-start = ((bf16[8,128,512]{2,1,0:T(8,128)(2,1)}), bf16[8,128,512]{2,1,0:T(8,128)(2,1)S(1)}, u32[]{:S(2)}, u32[]{:S(2)}) async-start(bf16[8,128,512]{2,1,0:T(8,128)(2,1)} %prepare.1), calls=%async_computation | async-start | bytes 2097152 | tf_op jit(solution)/shard_map/all_to_all | solution.py:246
  10.1 0.0 copy-done
  10.1 1.4 %collective-permute-start.4 = (bf16[512,256]{1,0:T(8,128)(2,1)S(1)}, bf16[512,256]{1,0:T(8,128)(2,1)}, u32[]{:S(2)}, u32[]{:S(2)}) collective-permute-start(bf16[512,256]{1,0:T(8,128)(2,1)S(1)} %get-tuple-element.33), channel_id=1, source_target_pairs={{56,40},{57,41},{58,42},{59,43},{60,44},{61,45},{62,46},{63,47}} | collective-permute-start | bytes 786440 | tf_op jit(solution)/shard_map/ppermute | solution.py:267
  11.5 1.4 %collective-permute-start.2 = (bf16[512,256]{1,0:T(8,128)(2,1)S(1)}, bf16[512,256]{1,0:T(8,128)(2,1)}, u32[]{:S(2)}, u32[]{:S(2)}) collective-permute-start(bf16[512,256]{1,0:T(8,128)(2,1)S(1)} %get-tuple-element.34), channel_id=1, source_target_pairs={{56,8},{57,9},{58,10},{59,11},{60,12},{61,13},{62,14},{63,15}} | collective-permute-start | bytes 786440 | tf_op jit(solution)/shard_map/ppermute | solution.py:267
  12.9 0.0 copy-done.3
  12.9 1.9 %collective-permute-start = (bf16[1024,256]{1,0:T(8,128)(2,1)S(1)}, bf16[1024,256]{1,0:T(8,128)(2,1)}, u32[]{:S(2)}, u32[]{:S(2)}) collective-permute-start(bf16[1024,256]{1,0:T(8,128)(2,1)S(1)} %copy-done.3), channel_id=1, source_target_pairs={{0,8},{8,16},{16,24},{24,32},{32,40},{40,48},{48,56},{56,64},{64,7... | collective-permute-start | bytes 1572872 | tf_op jit(solution)/shard_map/ppermute | solution.py:159
  14.8 4.4 %collective-permute-start.1 = (bf16[1024,256]{1,0:T(8,128)(2,1)S(1)}, bf16[1024,256]{1,0:T(8,128)(2,1)}, u32[]{:S(2)}, u32[]{:S(2)}) collective-permute-start(bf16[1024,256]{1,0:T(8,128)(2,1)S(1)} %copy-done), channel_id=1, source_target_pairs={{0,8},{8,16},{16,24},{24,32},{32,40},{40,48},{48,56},{64,72},{72,8... | collective-permute-start | bytes 1572872 | tf_op jit(solution)/shard_map/ppermute | solution.py:159
  19.2 0.0 collective-permute-done.4
  19.2 1.3 %collective-permute-start.5 = (bf16[512,256]{1,0:T(8,128)(2,1)}, bf16[512,256]{1,0:T(8,128)(2,1)S(1)}, u32[]{:S(2)}, u32[]{:S(2)}) collective-permute-start(bf16[512,256]{1,0:T(8,128)(2,1)} %collective-permute-done.4), channel_id=1, source_target_pairs={{40,64},{41,65},{42,66},{43,67},{44,68},{45,69},{46,70},{47,71}} | collective-permute-start | bytes 786440 | tf_op jit(solution)/shard_map/ppermute | solution.py:274
  20.5 0.0 collective-permute-done.2
  20.5 1.3 %collective-permute-start.3 = (bf16[512,256]{1,0:T(8,128)(2,1)}, bf16[512,256]{1,0:T(8,128)(2,1)}, u32[]{:S(2)}, u32[]{:S(2)}) collective-permute-start(bf16[512,256]{1,0:T(8,128)(2,1)} %collective-permute-done.2), channel_id=1, source_target_pairs={{8,64},{9,65},{10,66},{11,67},{12,68},{13,69},{14,70},{15,71}} | collective-permute-start | bytes 786440 | tf_op jit(solution)/shard_map/ppermute | solution.py:274
  21.8 10.1 %collective-permute-done.5.refs_8_ = bf16[512,256]{1,0:T(8,128)(2,1)S(1)} collective-permute-done((bf16[512,256]{1,0:T(8,128)(2,1)}, bf16[512,256]{1,0:T(8,128)(2,1)S(1)}, u32[]{:S(2)}, u32[]{:S(2)}) %collective-permute-start.5) | collective-permute-done | bytes 262176 | tf_op jit(solution)/shard_map/ppermute | solution.py:274
  31.9 0.0 collective-permute-done.3.refs_7_
  31.9 2.3 %collective-permute-done.refs_5_ = bf16[1024,256]{1,0:T(8,128)(2,1)} collective-permute-done((bf16[1024,256]{1,0:T(8,128)(2,1)S(1)}, bf16[1024,256]{1,0:T(8,128)(2,1)}, u32[]{:S(2)}, u32[]{:S(2)}) %collective-permute-start) | collective-permute-done | bytes 524320 | tf_op jit(solution)/shard_map/ppermute | solution.py:159
  34.3 0.0 collective-permute-done.1.refs_6_
  34.3 0.0 all-to-all-done
  34.3 0.0 copy-done.2
  34.3 0.0 copy-done.5
  34.3 0.0 copy-start.1
  34.3 0.0 copy-start.4
  34.3 10.5 %rim_band.1 = (f32[512,1024]{1,0:T(8,128)S(1)}, bf16[1024,512]{1,0:T(8,128)(2,1)}, f32[32,1024]{1,0:T(8,128)S(1)}) custom-call(f32[1]{0:T(128)} %bitcast.1.refs_0_, f32[4,1024]{1,0:T(4,128)S(1)} %copy-done.5, bf16[1024,512]{1,0:T(8,128)(2,1)} %refs_1_.3, bf16[1024,512]{1,0:T(8,128)(2,1)S(1)} %bitcast.7, bf16[1024,512]{1,0:T(8,128)(2,1)S(1)} %copy-done.2, ...), custom_call_target="tpu_custom_call" | custom-call | flops 4000000000 | bytes 8388608 | tf_op jit(solution)/shard_map/rim_band/pallas_call | solution.py:141
  44.8 1.9 %collective-permute-start.6 = (bf16[1024,512]{1,0:T(8,128)(2,1)}, bf16[1024,512]{1,0:T(8,128)(2,1)}, u32[]{:S(2)}, u32[]{:S(2)}) collective-permute-start(bf16[1024,512]{1,0:T(8,128)(2,1)} %get-tuple-element.22), channel_id=1, source_target_pairs={{8,0},{16,8},{24,16},{32,24},{40,32},{48,40},{56,48},{64,56},{72,6... | collective-permute-start | bytes 3145736 | tf_op jit(solution)/shard_map/ppermute | solution.py:159
  46.7 0.0 copy-done.1
  46.7 0.0 copy-done.4
  46.7 9.8 %own_band.1 = (bf16[1024,512]{1,0:T(8,128)(2,1)}, f32[1024,512]{1,0:T(8,128)S(1)}) custom-call(f32[4,1024]{1,0:T(4,128)S(1)} %copy-done.5, bf16[1024,512]{1,0:T(8,128)(2,1)} %refs_1_.3, bf16[1024,512]{1,0:T(8,128)(2,1)S(1)} %bitcast.8, f32[32,1024]{1,0:T(8,128)S(1)} %get-tuple-element.18.refs_3_, bf16[1024,256]{1,0:T(8,128)(2,1)S(1)} %copy-done.4, ...), custom_call_target="tpu_custom_call" | custom-call | flops 4000000000 | bytes 8388608 | tf_op jit(solution)/shard_map/own_band/pallas_call | solution.py:141
  56.5 6.4 %all-to-all-start.1 = ((bf16[8,128,512]{2,1,0:T(8,128)(2,1)}), bf16[8,128,512]{2,1,0:T(8,128)(2,1)}, u32[]{:S(2)}, u32[]{:S(2)}) async-start(bf16[8,128,512]{2,1,0:T(8,128)(2,1)} %bitcast.9), calls=%async_computation.1 | async-start | bytes 2097152 | tf_op jit(solution)/shard_map/all_to_all | solution.py:246
  62.9 0.0 collective-permute-done.6.later_ref
  62.9 1.4 %sum_parts.1 = (bf16[128,512]{1,0:T(8,128)(2,1)S(1)}, bf16[128,512]{1,0:T(8,128)(2,1)S(1)}, bf16[128,512]{1,0:T(8,128)(2,1)S(1)}, bf16[128,512]{1,0:T(8,128)(2,1...) custom-call(s32[1]{0:T(128)} %bitcast.4.me_ref, ...), custom_call_target="tpu_custom_call" | custom-call | flops 1000000 | bytes 4194304 | tf_op jit(solution)/shard_map/sum_parts/pallas_call | solution.py:206
  64.3 2.1 %collective-permute-start.7 = (bf16[128,512]{1,0:T(8,128)(2,1)S(1)}, bf16[128,512]{1,0:T(8,128)(2,1)S(1)}, u32[]{:S(2)}, u32[]{:S(2)}) collective-permute-start(bf16[128,512]{1,0:T(8,128)(2,1)S(1)} %get-tuple-element.24), channel_id=1, source_target_pairs={{0,2},{1,3},{2,4},{3,5},{4,6},{5,7},{6,0},{7,1},{8,10},{9,11},{10,... | collective-permute-start | bytes 393224 | tf_op jit(solution)/shard_map/ppermute | solution.py:255
  66.4 3.0 %collective-permute-start.8 = (bf16[128,512]{1,0:T(8,128)(2,1)S(1)}, bf16[128,512]{1,0:T(8,128)(2,1)S(1)}, u32[]{:S(2)}, u32[]{:S(2)}) collective-permute-start(bf16[128,512]{1,0:T(8,128)(2,1)S(1)} %get-tuple-element.25), channel_id=1, source_target_pairs={{0,1},{1,0},{2,3},{3,2},{4,5},{5,4},{6,7},{7,6},{8,9},{9,8},{10,11... | collective-permute-start | bytes 393224 | tf_op jit(solution)/shard_map/ppermute | solution.py:255
  69.4 1.8 %collective-permute-start.9 = (bf16[128,512]{1,0:T(8,128)(2,1)S(1)}, bf16[128,512]{1,0:T(8,128)(2,1)S(1)}, u32[]{:S(2)}, u32[]{:S(2)}) collective-permute-start(bf16[128,512]{1,0:T(8,128)(2,1)S(1)} %get-tuple-element.26), channel_id=1, source_target_pairs={{0,6},{1,7},{2,0},{3,1},{4,2},{5,3},{6,4},{7,5},{8,14},{9,15},{10,... | collective-permute-start | bytes 393224 | tf_op jit(solution)/shard_map/ppermute | solution.py:255
  71.1 1.8 %collective-permute-start.10 = (bf16[128,512]{1,0:T(8,128)(2,1)S(1)}, bf16[128,512]{1,0:T(8,128)(2,1)S(1)}, u32[]{:S(2)}, u32[]{:S(2)}) collective-permute-start(bf16[128,512]{1,0:T(8,128)(2,1)S(1)} %get-tuple-element.27), channel_id=1, source_target_pairs={{0,5},{1,4},{2,7},{3,6},{4,1},{5,0},{6,3},{7,2},{8,13},{9,12},{10,... | collective-permute-start | bytes 393224 | tf_op jit(solution)/shard_map/ppermute | solution.py:255
  72.9 1.3 %collective-permute-start.11 = (bf16[128,512]{1,0:T(8,128)(2,1)S(1)}, bf16[128,512]{1,0:T(8,128)(2,1)S(1)}, u32[]{:S(2)}, u32[]{:S(2)}) collective-permute-start(bf16[128,512]{1,0:T(8,128)(2,1)S(1)} %get-tuple-element.28), channel_id=1, source_target_pairs={{0,4},{1,5},{2,6},{3,7},{4,0},{5,1},{6,2},{7,3},{8,12},{9,13},{10,... | collective-permute-start | bytes 393224 | tf_op jit(solution)/shard_map/ppermute | solution.py:255
  74.2 7.6 %collective-permute-done.7.refs_1_ = bf16[128,512]{1,0:T(8,128)(2,1)S(1)} collective-permute-done((bf16[128,512]{1,0:T(8,128)(2,1)S(1)}, bf16[128,512]{1,0:T(8,128)(2,1)S(1)}, u32[]{:S(2)}, u32[]{:S(2)}) %collective-permute-start.7) | collective-permute-done | bytes 131104 | tf_op jit(solution)/shard_map/ppermute | solution.py:255
  81.8 4.8 %collective-permute-start.12 = (bf16[128,512]{1,0:T(8,128)(2,1)S(1)}, bf16[128,512]{1,0:T(8,128)(2,1)S(1)}, u32[]{:S(2)}, u32[]{:S(2)}) collective-permute-start(bf16[128,512]{1,0:T(8,128)(2,1)S(1)} %get-tuple-element.29), channel_id=1, source_target_pairs={{0,3},{1,2},{2,5},{3,4},{4,7},{5,6},{6,1},{7,0},{8,11},{9,10},{10,... | collective-permute-start | bytes 393224 | tf_op jit(solution)/shard_map/ppermute | solution.py:255
  86.6 0.0 collective-permute-done.8.refs_2_
  86.7 1.3 %collective-permute-start.13 = (bf16[128,512]{1,0:T(8,128)(2,1)S(1)}, bf16[128,512]{1,0:T(8,128)(2,1)S(1)}, u32[]{:S(2)}, u32[]{:S(2)}) collective-permute-start(bf16[128,512]{1,0:T(8,128)(2,1)S(1)} %get-tuple-element.30), channel_id=1, source_target_pairs={{0,7},{1,6},{2,1},{3,0},{4,3},{5,2},{6,5},{7,4},{8,15},{9,14},{10,... | collective-permute-start | bytes 393224 | tf_op jit(solution)/shard_map/ppermute | solution.py:255
  88.0 0.0 all-to-all-done.1
  88.0 2.3 %copy.10 = bf16[8,16,8,512]{3,2,0,1:T(8,128)(2,1)} copy(bf16[8,16,8,512]{3,2,1,0:T(8,128)(2,1)} %bitcast.5) | data formatting | bytes 2097152 | tf_op jit(solution)/shard_map/reshape | solution.py:285
  90.3 0.0 collective-permute-done.9.refs_3_
  90.3 0.0 collective-permute-done.10.refs_4_
  90.3 0.0 collective-permute-done.11.refs_5_
  90.3 1.0 %collective-permute-done.12.refs_6_ = bf16[128,512]{1,0:T(8,128)(2,1)S(1)} collective-permute-done((bf16[128,512]{1,0:T(8,128)(2,1)S(1)}, bf16[128,512]{1,0:T(8,128)(2,1)S(1)}, u32[]{:S(2)}, u32[]{:S(2)}) %collective-permute-start.12) | collective-permute-done | bytes 131104 | tf_op jit(solution)/shard_map/ppermute | solution.py:255
  91.3 2.7 %collective-permute-done.13.refs_7_ = bf16[128,512]{1,0:T(8,128)(2,1)S(1)} collective-permute-done((bf16[128,512]{1,0:T(8,128)(2,1)S(1)}, bf16[128,512]{1,0:T(8,128)(2,1)S(1)}, u32[]{:S(2)}, u32[]{:S(2)}) %collective-permute-start.13) | collective-permute-done | bytes 131104 | tf_op jit(solution)/shard_map/ppermute | solution.py:255
  94.0 1.3 %join.1 = (bf16[128,2048]{1,0:T(8,128)(2,1)}, bf16[128,2048]{1,0:T(8,128)(2,1)}) custom-call(s32[1]{0:T(128)} %bitcast.4.me_ref, bf16[128,512]{1,0:T(8,128)(2,1)S(1)} %get-tuple-element.23.refs_0_, bf16[128,512]{1,0:T(8,128)(2,1)S(1)} %collective-permute-done.7.refs_1_, bf16[128,512]{1,0:T(8,128)(2,1)S(1)} %collective-permute-done.8.refs_2_, ...), custom_call_target="tpu_custom_call" | custom-call | bytes 4194304 | tf_op jit(solution)/shard_map/join/pallas_call | solution.py:232
  (1 shorter events, 0.0 us)
Async XLA Ops:
  0.6 9.5 %copy-start = (bf16[1024,256]{1,0:T(8,128)(2,1)S(1)}, bf16[1024,256]{1,0:T(8,128)(2,1)}, u32[]{:S(2)}) copy-start(bf16[1024,256]{1,0:T(8,128)(2,1)} %refs_5_.1) | copy-start | bytes 1572868
  3.0 9.9 %copy-start.3 = (bf16[1024,256]{1,0:T(8,128)(2,1)S(1)}, bf16[1024,256]{1,0:T(8,128)(2,1)}, u32[]{:S(2)}) copy-start(bf16[1024,256]{1,0:T(8,128)(2,1)} %refs_4_.3) | copy-start | bytes 1572868
  3.0 31.2 %copy-start.2 = (bf16[1024,512]{1,0:T(8,128)(2,1)S(1)}, bf16[1024,512]{1,0:T(8,128)(2,1)}, u32[]{:S(2)}) copy-start(bf16[1024,512]{1,0:T(8,128)(2,1)} %refs_4_.2) | copy-start | bytes 3145732
  3.0 31.2 %copy-start.5 = (f32[4,1024]{1,0:T(4,128)S(1)}, f32[4,1024]{1,0:T(4,128)}, u32[]{:S(2)}) copy-start(f32[4,1024]{1,0:T(4,128)} %refs_0_.1) | copy-start | bytes 49156
  3.1 31.2 %all-to-all-start = ((bf16[8,128,512]{2,1,0:T(8,128)(2,1)}), bf16[8,128,512]{2,1,0:T(8,128)(2,1)S(1)}, u32[]{:S(2)}, u32[]{:S(2)}) async-start(bf16[8,128,512]{2,1,0:T(8,128)(2,1)} %prepare.1), calls=%async_computation | async-start | bytes 2097152 | tf_op jit(solution)/shard_map/all_to_all | solution.py:246
  10.1 9.1 %collective-permute-start.4 = (bf16[512,256]{1,0:T(8,128)(2,1)S(1)}, bf16[512,256]{1,0:T(8,128)(2,1)}, u32[]{:S(2)}, u32[]{:S(2)}) collective-permute-start(bf16[512,256]{1,0:T(8,128)(2,1)S(1)} %get-tuple-element.33), channel_id=1, source_target_pairs={{56,40},{57,41},{58,42},{59,43},{60,44},{61,45},{62,46},{63,47}} | collective-permute-start | bytes 786440 | tf_op jit(solution)/shard_map/ppermute | solution.py:267
  11.5 9.0 %collective-permute-start.2 = (bf16[512,256]{1,0:T(8,128)(2,1)S(1)}, bf16[512,256]{1,0:T(8,128)(2,1)}, u32[]{:S(2)}, u32[]{:S(2)}) collective-permute-start(bf16[512,256]{1,0:T(8,128)(2,1)S(1)} %get-tuple-element.34), channel_id=1, source_target_pairs={{56,8},{57,9},{58,10},{59,11},{60,12},{61,13},{62,14},{63,15}} | collective-permute-start | bytes 786440 | tf_op jit(solution)/shard_map/ppermute | solution.py:267
  12.9 21.4 %collective-permute-start = (bf16[1024,256]{1,0:T(8,128)(2,1)S(1)}, bf16[1024,256]{1,0:T(8,128)(2,1)}, u32[]{:S(2)}, u32[]{:S(2)}) collective-permute-start(bf16[1024,256]{1,0:T(8,128)(2,1)S(1)} %copy-done.3), channel_id=1, source_target_pairs={{0,8},{8,16},{16,24},{24,32},{32,40},{40,48},{48,56},{56,64},{64,7... | collective-permute-start | bytes 1572872 | tf_op jit(solution)/shard_map/ppermute | solution.py:159
  14.8 19.5 %collective-permute-start.1 = (bf16[1024,256]{1,0:T(8,128)(2,1)S(1)}, bf16[1024,256]{1,0:T(8,128)(2,1)}, u32[]{:S(2)}, u32[]{:S(2)}) collective-permute-start(bf16[1024,256]{1,0:T(8,128)(2,1)S(1)} %copy-done), channel_id=1, source_target_pairs={{0,8},{8,16},{16,24},{24,32},{32,40},{40,48},{48,56},{64,72},{72,8... | collective-permute-start | bytes 1572872 | tf_op jit(solution)/shard_map/ppermute | solution.py:159
  19.2 12.7 %collective-permute-start.5 = (bf16[512,256]{1,0:T(8,128)(2,1)}, bf16[512,256]{1,0:T(8,128)(2,1)S(1)}, u32[]{:S(2)}, u32[]{:S(2)}) collective-permute-start(bf16[512,256]{1,0:T(8,128)(2,1)} %collective-permute-done.4), channel_id=1, source_target_pairs={{40,64},{41,65},{42,66},{43,67},{44,68},{45,69},{46,70},{47,71}} | collective-permute-start | bytes 786440 | tf_op jit(solution)/shard_map/ppermute | solution.py:274
  20.5 11.4 %collective-permute-start.3 = (bf16[512,256]{1,0:T(8,128)(2,1)}, bf16[512,256]{1,0:T(8,128)(2,1)}, u32[]{:S(2)}, u32[]{:S(2)}) collective-permute-start(bf16[512,256]{1,0:T(8,128)(2,1)} %collective-permute-done.2), channel_id=1, source_target_pairs={{8,64},{9,65},{10,66},{11,67},{12,68},{13,69},{14,70},{15,71}} | collective-permute-start | bytes 786440 | tf_op jit(solution)/shard_map/ppermute | solution.py:274
  34.3 12.4 %copy-start.1 = (bf16[1024,256]{1,0:T(8,128)(2,1)S(1)}, bf16[1024,256]{1,0:T(8,128)(2,1)}, u32[]{:S(2)}) copy-start(bf16[1024,256]{1,0:T(8,128)(2,1)} %refs_5_.1) | copy-start | bytes 1572868
  34.3 12.4 %copy-start.4 = (bf16[1024,256]{1,0:T(8,128)(2,1)S(1)}, bf16[1024,256]{1,0:T(8,128)(2,1)}, u32[]{:S(2)}) copy-start(bf16[1024,256]{1,0:T(8,128)(2,1)} %refs_4_.3) | copy-start | bytes 1572868
  44.8 18.1 %collective-permute-start.6 = (bf16[1024,512]{1,0:T(8,128)(2,1)}, bf16[1024,512]{1,0:T(8,128)(2,1)}, u32[]{:S(2)}, u32[]{:S(2)}) collective-permute-start(bf16[1024,512]{1,0:T(8,128)(2,1)} %get-tuple-element.22), channel_id=1, source_target_pairs={{8,0},{16,8},{24,16},{32,24},{40,32},{48,40},{56,48},{64,56},{72,6... | collective-permute-start | bytes 3145736 | tf_op jit(solution)/shard_map/ppermute | solution.py:159
  56.5 31.5 %all-to-all-start.1 = ((bf16[8,128,512]{2,1,0:T(8,128)(2,1)}), bf16[8,128,512]{2,1,0:T(8,128)(2,1)}, u32[]{:S(2)}, u32[]{:S(2)}) async-start(bf16[8,128,512]{2,1,0:T(8,128)(2,1)} %bitcast.9), calls=%async_computation.1 | async-start | bytes 2097152 | tf_op jit(solution)/shard_map/all_to_all | solution.py:246
  64.3 17.5 %collective-permute-start.7 = (bf16[128,512]{1,0:T(8,128)(2,1)S(1)}, bf16[128,512]{1,0:T(8,128)(2,1)S(1)}, u32[]{:S(2)}, u32[]{:S(2)}) collective-permute-start(bf16[128,512]{1,0:T(8,128)(2,1)S(1)} %get-tuple-element.24), channel_id=1, source_target_pairs={{0,2},{1,3},{2,4},{3,5},{4,6},{5,7},{6,0},{7,1},{8,10},{9,11},{10,... | collective-permute-start | bytes 393224 | tf_op jit(solution)/shard_map/ppermute | solution.py:255
  66.4 20.3 %collective-permute-start.8 = (bf16[128,512]{1,0:T(8,128)(2,1)S(1)}, bf16[128,512]{1,0:T(8,128)(2,1)S(1)}, u32[]{:S(2)}, u32[]{:S(2)}) collective-permute-start(bf16[128,512]{1,0:T(8,128)(2,1)S(1)} %get-tuple-element.25), channel_id=1, source_target_pairs={{0,1},{1,0},{2,3},{3,2},{4,5},{5,4},{6,7},{7,6},{8,9},{9,8},{10,11... | collective-permute-start | bytes 393224 | tf_op jit(solution)/shard_map/ppermute | solution.py:255
  69.4 20.9 %collective-permute-start.9 = (bf16[128,512]{1,0:T(8,128)(2,1)S(1)}, bf16[128,512]{1,0:T(8,128)(2,1)S(1)}, u32[]{:S(2)}, u32[]{:S(2)}) collective-permute-start(bf16[128,512]{1,0:T(8,128)(2,1)S(1)} %get-tuple-element.26), channel_id=1, source_target_pairs={{0,6},{1,7},{2,0},{3,1},{4,2},{5,3},{6,4},{7,5},{8,14},{9,15},{10,... | collective-permute-start | bytes 393224 | tf_op jit(solution)/shard_map/ppermute | solution.py:255
  71.1 19.2 %collective-permute-start.10 = (bf16[128,512]{1,0:T(8,128)(2,1)S(1)}, bf16[128,512]{1,0:T(8,128)(2,1)S(1)}, u32[]{:S(2)}, u32[]{:S(2)}) collective-permute-start(bf16[128,512]{1,0:T(8,128)(2,1)S(1)} %get-tuple-element.27), channel_id=1, source_target_pairs={{0,5},{1,4},{2,7},{3,6},{4,1},{5,0},{6,3},{7,2},{8,13},{9,12},{10,... | collective-permute-start | bytes 393224 | tf_op jit(solution)/shard_map/ppermute | solution.py:255
  72.9 17.4 %collective-permute-start.11 = (bf16[128,512]{1,0:T(8,128)(2,1)S(1)}, bf16[128,512]{1,0:T(8,128)(2,1)S(1)}, u32[]{:S(2)}, u32[]{:S(2)}) collective-permute-start(bf16[128,512]{1,0:T(8,128)(2,1)S(1)} %get-tuple-element.28), channel_id=1, source_target_pairs={{0,4},{1,5},{2,6},{3,7},{4,0},{5,1},{6,2},{7,3},{8,12},{9,13},{10,... | collective-permute-start | bytes 393224 | tf_op jit(solution)/shard_map/ppermute | solution.py:255
  81.8 9.5 %collective-permute-start.12 = (bf16[128,512]{1,0:T(8,128)(2,1)S(1)}, bf16[128,512]{1,0:T(8,128)(2,1)S(1)}, u32[]{:S(2)}, u32[]{:S(2)}) collective-permute-start(bf16[128,512]{1,0:T(8,128)(2,1)S(1)} %get-tuple-element.29), channel_id=1, source_target_pairs={{0,3},{1,2},{2,5},{3,4},{4,7},{5,6},{6,1},{7,0},{8,11},{9,10},{10,... | collective-permute-start | bytes 393224 | tf_op jit(solution)/shard_map/ppermute | solution.py:255
  86.7 7.4 %collective-permute-start.13 = (bf16[128,512]{1,0:T(8,128)(2,1)S(1)}, bf16[128,512]{1,0:T(8,128)(2,1)S(1)}, u32[]{:S(2)}, u32[]{:S(2)}) collective-permute-start(bf16[128,512]{1,0:T(8,128)(2,1)S(1)} %get-tuple-element.30), channel_id=1, source_target_pairs={{0,7},{1,6},{2,1},{3,0},{4,3},{5,2},{6,5},{7,4},{8,15},{9,14},{10,... | collective-permute-start | bytes 393224 | tf_op jit(solution)/shard_map/ppermute | solution.py:255

commit v3 on v2

--- a/solution.py
+++ b/solution.py
@@ -260,7 +260,7 @@
     me = lax.axis_index("head").astype(jnp.int32).reshape(1)
     edge = jnp.where(lax.axis_index("seq") == 0, BIG, 0.0).astype(jnp.float32).reshape(1)
     half = lax.axis_size("seq") // 2
-    middle = (1, half - 3)
+    middle = (1, half - 5)
     detours = []
     for n in range(2):
         rows = value_states[n * TOK // 2 : (n + 1) * TOK // 2]
@@ -272,9 +272,9 @@
     v_far = []
     for n in range(2):
         v_far.append(lax.ppermute(detours[n], "seq", [(middle[n], half)]))
-    queries = pltpu.with_memory_space_constraint(queries, pltpu.HBM)
+    queries_rim = pltpu.with_memory_space_constraint(queries, pltpu.HBM)
     part, rim, delta = band(
-        False, edge, log_norm, queries, grad_local, outputs, k_rim, v_rim, *v_far
+        False, edge, log_norm, queries_rim, grad_local, outputs, k_rim, v_rim, *v_far
     )
     later = from_behind(rim, -1)
     dq, own = band(True, log_norm, queries, grad_local, delta, key_states, value_states, part)

time: 96.3 us -> 93.3 us (0.969)
  waiting for transfers between devices: 23.8 us -> 21.1 us
    ppermute x2, waiting for transfers between devices: 10.1 us -> 6.7 us  [on_device(): v_far.append(lax.ppermute(detours[n], 'seq', [(middle[n], half)]))]
  transfers between devices with their start and end apart: 16 -> 16, of which waited for: 5 -> 6; matrix products, arithmetic and copies ran while one was open for 2% -> 3% of each run, Pallas kernels for 12% -> 11%
where the time goes in v3:
time: 93.3 us; the launch traced here: 91.9 us
  starting transfers between devices  42.9 us (46%)
  Pallas kernels  24.6 us (26%)
  waiting for transfers between devices  21.1 us (23%)
  local copies, waits for them, and re-layouts  2.39 us (3%)
    pallas_call x2, Pallas kernels, band(): pl.pallas_call(functools.partial(band_kernel, own), name='own_band' if ow...  19.6 us
    ppermute x7, starting transfers between devices, shift_heads(): return lax.ppermute(x, 'head', [(i, partner(i, hop)) for i in range(8)])  16 us
    all_to_all x2, starting transfers between devices, exchange(): lax.all_to_all(parts, 'head', split_axis=0, concat_axis=0, tiled=True)  13.3 us
    ppermute x7, waiting for transfers between devices, shift_heads(): return lax.ppermute(x, 'head', [(i, partner(i, hop)) for i in range(8)])  11.4 us
    ppermute x3, starting transfers between devices, from_behind(): return lax.ppermute(shard, 'seq', pairs)  8.23 us
    ppermute x2, waiting for transfers between devices, on_device(): v_far.append(lax.ppermute(detours[n], 'seq', [(middle[n], half)]))  6.7 us
    ppermute x3, waiting for transfers between devices, from_behind(): return lax.ppermute(shard, 'seq', pairs)  3.02 us
    ppermute x2, starting transfers between devices, on_device(): detours.append(lax.ppermute(rows, 'seq', [(half - 1, middle[n])]))  2.75 us
  transfers between devices with their start and end apart: 16, of which 6 were waited for; matrix products, arithmetic and copies ran while one was open for 3% of the time, Pallas kernels for 11%

profile of v3, /device:TPU:2, one launch (start us, length us, event | category | flops | bytes accessed | tf_op | source)
XLA Modules:
  0.0 91.9 jit_solution(13507552758815763371)
XLA Ops:
  0.6 0.0 copy-start
  0.6 2.4 %prepare.1 = bf16[8,128,512]{2,1,0:T(8,128)(2,1)} custom-call(bf16[128,4096]{1,0:T(8,128)(2,1)} %g_ref.1), custom_call_target="tpu_custom_call" | custom-call | bytes 2097152 | tf_op jit(solution)/shard_map/prepare/pallas_call | solution.py:178
  3.0 0.0 copy-start.4
  3.0 0.0 copy-start.2
  3.0 0.0 copy-start.6
  3.1 7.0 %all-to-all-start = ((bf16[8,128,512]{2,1,0:T(8,128)(2,1)}), bf16[8,128,512]{2,1,0:T(8,128)(2,1)S(1)}, u32[]{:S(2)}, u32[]{:S(2)}) async-start(bf16[8,128,512]{2,1,0:T(8,128)(2,1)} %prepare.1), calls=%async_computation | async-start | bytes 2097152 | tf_op jit(solution)/shard_map/all_to_all | solution.py:246
  10.1 0.0 copy-done
  10.1 1.4 %collective-permute-start.4 = (bf16[512,256]{1,0:T(8,128)(2,1)S(1)}, bf16[512,256]{1,0:T(8,128)(2,1)}, u32[]{:S(2)}, u32[]{:S(2)}) collective-permute-start(bf16[512,256]{1,0:T(8,128)(2,1)S(1)} %get-tuple-element.33), channel_id=1, source_target_pairs={{56,24},{57,25},{58,26},{59,27},{60,28},{61,29},{62,30},{63,31}} | collective-permute-start | bytes 786440 | tf_op jit(solution)/shard_map/ppermute | solution.py:267
  11.5 1.4 %collective-permute-start.2 = (bf16[512,256]{1,0:T(8,128)(2,1)S(1)}, bf16[512,256]{1,0:T(8,128)(2,1)}, u32[]{:S(2)}, u32[]{:S(2)}) collective-permute-start(bf16[512,256]{1,0:T(8,128)(2,1)S(1)} %get-tuple-element.34), channel_id=1, source_target_pairs={{56,8},{57,9},{58,10},{59,11},{60,12},{61,13},{62,14},{63,15}} | collective-permute-start | bytes 786440 | tf_op jit(solution)/shard_map/ppermute | solution.py:267
  12.9 0.0 copy-done.4
  12.9 1.9 %collective-permute-start = (bf16[1024,256]{1,0:T(8,128)(2,1)S(1)}, bf16[1024,256]{1,0:T(8,128)(2,1)}, u32[]{:S(2)}, u32[]{:S(2)}) collective-permute-start(bf16[1024,256]{1,0:T(8,128)(2,1)S(1)} %copy-done.4), channel_id=1, source_target_pairs={{0,8},{8,16},{16,24},{24,32},{32,40},{40,48},{48,56},{56,64},{64,7... | collective-permute-start | bytes 1572872 | tf_op jit(solution)/shard_map/ppermute | solution.py:159
  14.8 4.4 %collective-permute-start.1 = (bf16[1024,256]{1,0:T(8,128)(2,1)S(1)}, bf16[1024,256]{1,0:T(8,128)(2,1)}, u32[]{:S(2)}, u32[]{:S(2)}) collective-permute-start(bf16[1024,256]{1,0:T(8,128)(2,1)S(1)} %copy-done), channel_id=1, source_target_pairs={{0,8},{8,16},{16,24},{24,32},{32,40},{40,48},{48,56},{64,72},{72,8... | collective-permute-start | bytes 1572872 | tf_op jit(solution)/shard_map/ppermute | solution.py:159
  19.2 0.0 collective-permute-done.4
  19.2 1.3 %collective-permute-start.5 = (bf16[512,256]{1,0:T(8,128)(2,1)}, bf16[512,256]{1,0:T(8,128)(2,1)S(1)}, u32[]{:S(2)}, u32[]{:S(2)}) collective-permute-start(bf16[512,256]{1,0:T(8,128)(2,1)} %collective-permute-done.4), channel_id=1, source_target_pairs={{24,64},{25,65},{26,66},{27,67},{28,68},{29,69},{30,70},{31,71}} | collective-permute-start | bytes 786440 | tf_op jit(solution)/shard_map/ppermute | solution.py:274
  20.5 0.0 collective-permute-done.2
  20.5 1.3 %collective-permute-start.3 = (bf16[512,256]{1,0:T(8,128)(2,1)}, bf16[512,256]{1,0:T(8,128)(2,1)}, u32[]{:S(2)}, u32[]{:S(2)}) collective-permute-start(bf16[512,256]{1,0:T(8,128)(2,1)} %collective-permute-done.2), channel_id=1, source_target_pairs={{8,64},{9,65},{10,66},{11,67},{12,68},{13,69},{14,70},{15,71}} | collective-permute-start | bytes 786440 | tf_op jit(solution)/shard_map/ppermute | solution.py:274
  21.8 6.2 %collective-permute-done.5.refs_8_ = bf16[512,256]{1,0:T(8,128)(2,1)S(1)} collective-permute-done((bf16[512,256]{1,0:T(8,128)(2,1)}, bf16[512,256]{1,0:T(8,128)(2,1)S(1)}, u32[]{:S(2)}, u32[]{:S(2)}) %collective-permute-start.5) | collective-permute-done | bytes 262176 | tf_op jit(solution)/shard_map/ppermute | solution.py:274
  28.0 0.5 collective-permute-done.3.refs_7_
  28.5 3.0 %collective-permute-done.refs_5_ = bf16[1024,256]{1,0:T(8,128)(2,1)} collective-permute-done((bf16[1024,256]{1,0:T(8,128)(2,1)S(1)}, bf16[1024,256]{1,0:T(8,128)(2,1)}, u32[]{:S(2)}, u32[]{:S(2)}) %collective-permute-start) | collective-permute-done | bytes 524320 | tf_op jit(solution)/shard_map/ppermute | solution.py:159
  31.5 0.0 collective-permute-done.1.refs_6_
  31.5 0.0 all-to-all-done
  31.5 0.0 copy-done.2
  31.5 0.0 copy-done.6
  31.6 0.0 copy-start.1
  31.6 0.0 copy-start.3
  31.6 0.0 copy-start.5
  31.6 10.5 %rim_band.1 = (f32[512,1024]{1,0:T(8,128)S(1)}, bf16[1024,512]{1,0:T(8,128)(2,1)}, f32[32,1024]{1,0:T(8,128)S(1)}) custom-call(f32[1]{0:T(128)} %bitcast.1.refs_0_, f32[4,1024]{1,0:T(4,128)S(1)} %copy-done.6, bf16[1024,512]{1,0:T(8,128)(2,1)} %refs_1_.3, bf16[1024,512]{1,0:T(8,128)(2,1)S(1)} %bitcast.7, bf16[1024,512]{1,0:T(8,128)(2,1)S(1)} %copy-done.2, ...), custom_call_target="tpu_custom_call" | custom-call | flops 4000000000 | bytes 8388608 | tf_op jit(solution)/shard_map/rim_band/pallas_call | solution.py:141
  42.1 1.9 %collective-permute-start.6 = (bf16[1024,512]{1,0:T(8,128)(2,1)}, bf16[1024,512]{1,0:T(8,128)(2,1)}, u32[]{:S(2)}, u32[]{:S(2)}) collective-permute-start(bf16[1024,512]{1,0:T(8,128)(2,1)} %get-tuple-element.22), channel_id=1, source_target_pairs={{8,0},{16,8},{24,16},{32,24},{40,32},{48,40},{56,48},{64,56},{72,6... | collective-permute-start | bytes 3145736 | tf_op jit(solution)/shard_map/ppermute | solution.py:159
  44.0 0.0 copy-done.1
  44.0 0.0 copy-done.3
  44.0 0.0 copy-done.5
  44.1 9.1 %own_band.1 = (bf16[1024,512]{1,0:T(8,128)(2,1)}, f32[1024,512]{1,0:T(8,128)S(1)}) custom-call(f32[4,1024]{1,0:T(4,128)S(1)} %copy-done.6, bf16[1024,512]{1,0:T(8,128)(2,1)S(1)} %copy-done.3, bf16[1024,512]{1,0:T(8,128)(2,1)S(1)} %bitcast.8, f32[32,1024]{1,0:T(8,128)S(1)} %get-tuple-element.18.refs_3_, bf16[1024,256]{1,0:T(8,128)(2,1)S(1)} %copy-done.5, ...), custom_call_target="tpu_custom_call" | custom-call | flops 4000000000 | bytes 8388608 | tf_op jit(solution)/shard_map/own_band/pallas_call | solution.py:141
  53.1 6.3 %all-to-all-start.1 = ((bf16[8,128,512]{2,1,0:T(8,128)(2,1)}), bf16[8,128,512]{2,1,0:T(8,128)(2,1)}, u32[]{:S(2)}, u32[]{:S(2)}) async-start(bf16[8,128,512]{2,1,0:T(8,128)(2,1)} %bitcast.9), calls=%async_computation.1 | async-start | bytes 2097152 | tf_op jit(solution)/shard_map/all_to_all | solution.py:246
  59.5 0.0 collective-permute-done.6.later_ref
  59.5 1.4 %sum_parts.1 = (bf16[128,512]{1,0:T(8,128)(2,1)S(1)}, bf16[128,512]{1,0:T(8,128)(2,1)S(1)}, bf16[128,512]{1,0:T(8,128)(2,1)S(1)}, bf16[128,512]{1,0:T(8,128)(2,1...) custom-call(s32[1]{0:T(128)} %bitcast.4.me_ref, ...), custom_call_target="tpu_custom_call" | custom-call | flops 1000000 | bytes 4194304 | tf_op jit(solution)/shard_map/sum_parts/pallas_call | solution.py:206
  60.9 2.1 %collective-permute-start.7 = (bf16[128,512]{1,0:T(8,128)(2,1)S(1)}, bf16[128,512]{1,0:T(8,128)(2,1)S(1)}, u32[]{:S(2)}, u32[]{:S(2)}) collective-permute-start(bf16[128,512]{1,0:T(8,128)(2,1)S(1)} %get-tuple-element.24), channel_id=1, source_target_pairs={{0,2},{1,3},{2,4},{3,5},{4,6},{5,7},{6,0},{7,1},{8,10},{9,11},{10,... | collective-permute-start | bytes 393224 | tf_op jit(solution)/shard_map/ppermute | solution.py:255
  63.0 3.0 %collective-permute-start.8 = (bf16[128,512]{1,0:T(8,128)(2,1)S(1)}, bf16[128,512]{1,0:T(8,128)(2,1)S(1)}, u32[]{:S(2)}, u32[]{:S(2)}) collective-permute-start(bf16[128,512]{1,0:T(8,128)(2,1)S(1)} %get-tuple-element.25), channel_id=1, source_target_pairs={{0,1},{1,0},{2,3},{3,2},{4,5},{5,4},{6,7},{7,6},{8,9},{9,8},{10,11... | collective-permute-start | bytes 393224 | tf_op jit(solution)/shard_map/ppermute | solution.py:255
  65.9 1.8 %collective-permute-start.9 = (bf16[128,512]{1,0:T(8,128)(2,1)S(1)}, bf16[128,512]{1,0:T(8,128)(2,1)S(1)}, u32[]{:S(2)}, u32[]{:S(2)}) collective-permute-start(bf16[128,512]{1,0:T(8,128)(2,1)S(1)} %get-tuple-element.26), channel_id=1, source_target_pairs={{0,6},{1,7},{2,0},{3,1},{4,2},{5,3},{6,4},{7,5},{8,14},{9,15},{10,... | collective-permute-start | bytes 393224 | tf_op jit(solution)/shard_map/ppermute | solution.py:255
  67.7 1.8 %collective-permute-start.10 = (bf16[128,512]{1,0:T(8,128)(2,1)S(1)}, bf16[128,512]{1,0:T(8,128)(2,1)S(1)}, u32[]{:S(2)}, u32[]{:S(2)}) collective-permute-start(bf16[128,512]{1,0:T(8,128)(2,1)S(1)} %get-tuple-element.27), channel_id=1, source_target_pairs={{0,5},{1,4},{2,7},{3,6},{4,1},{5,0},{6,3},{7,2},{8,13},{9,12},{10,... | collective-permute-start | bytes 393224 | tf_op jit(solution)/shard_map/ppermute | solution.py:255
  69.5 1.3 %collective-permute-start.11 = (bf16[128,512]{1,0:T(8,128)(2,1)S(1)}, bf16[128,512]{1,0:T(8,128)(2,1)S(1)}, u32[]{:S(2)}, u32[]{:S(2)}) collective-permute-start(bf16[128,512]{1,0:T(8,128)(2,1)S(1)} %get-tuple-element.28), channel_id=1, source_target_pairs={{0,4},{1,5},{2,6},{3,7},{4,0},{5,1},{6,2},{7,3},{8,12},{9,13},{10,... | collective-permute-start | bytes 393224 | tf_op jit(solution)/shard_map/ppermute | solution.py:255
  70.8 7.6 %collective-permute-done.7.refs_1_ = bf16[128,512]{1,0:T(8,128)(2,1)S(1)} collective-permute-done((bf16[128,512]{1,0:T(8,128)(2,1)S(1)}, bf16[128,512]{1,0:T(8,128)(2,1)S(1)}, u32[]{:S(2)}, u32[]{:S(2)}) %collective-permute-start.7) | collective-permute-done | bytes 131104 | tf_op jit(solution)/shard_map/ppermute | solution.py:255
  78.4 4.8 %collective-permute-start.12 = (bf16[128,512]{1,0:T(8,128)(2,1)S(1)}, bf16[128,512]{1,0:T(8,128)(2,1)S(1)}, u32[]{:S(2)}, u32[]{:S(2)}) collective-permute-start(bf16[128,512]{1,0:T(8,128)(2,1)S(1)} %get-tuple-element.29), channel_id=1, source_target_pairs={{0,3},{1,2},{2,5},{3,4},{4,7},{5,6},{6,1},{7,0},{8,11},{9,10},{10,... | collective-permute-start | bytes 393224 | tf_op jit(solution)/shard_map/ppermute | solution.py:255
  83.2 0.0 collective-permute-done.8.refs_2_
  83.2 1.3 %collective-permute-start.13 = (bf16[128,512]{1,0:T(8,128)(2,1)S(1)}, bf16[128,512]{1,0:T(8,128)(2,1)S(1)}, u32[]{:S(2)}, u32[]{:S(2)}) collective-permute-start(bf16[128,512]{1,0:T(8,128)(2,1)S(1)} %get-tuple-element.30), channel_id=1, source_target_pairs={{0,7},{1,6},{2,1},{3,0},{4,3},{5,2},{6,5},{7,4},{8,15},{9,14},{10,... | collective-permute-start | bytes 393224 | tf_op jit(solution)/shard_map/ppermute | solution.py:255
  84.6 0.0 all-to-all-done.1
  84.6 2.3 %copy.10 = bf16[8,16,8,512]{3,2,0,1:T(8,128)(2,1)} copy(bf16[8,16,8,512]{3,2,1,0:T(8,128)(2,1)} %bitcast.5) | data formatting | bytes 2097152 | tf_op jit(solution)/shard_map/reshape | solution.py:285
  86.9 0.0 collective-permute-done.9.refs_3_
  86.9 0.0 collective-permute-done.10.refs_4_
  86.9 0.0 collective-permute-done.11.refs_5_
  86.9 1.0 %collective-permute-done.12.refs_6_ = bf16[128,512]{1,0:T(8,128)(2,1)S(1)} collective-permute-done((bf16[128,512]{1,0:T(8,128)(2,1)S(1)}, bf16[128,512]{1,0:T(8,128)(2,1)S(1)}, u32[]{:S(2)}, u32[]{:S(2)}) %collective-permute-start.12) | collective-permute-done | bytes 131104 | tf_op jit(solution)/shard_map/ppermute | solution.py:255
  87.9 2.7 %collective-permute-done.13.refs_7_ = bf16[128,512]{1,0:T(8,128)(2,1)S(1)} collective-permute-done((bf16[128,512]{1,0:T(8,128)(2,1)S(1)}, bf16[128,512]{1,0:T(8,128)(2,1)S(1)}, u32[]{:S(2)}, u32[]{:S(2)}) %collective-permute-start.13) | collective-permute-done | bytes 131104 | tf_op jit(solution)/shard_map/ppermute | solution.py:255
  90.6 1.3 %join.1 = (bf16[128,2048]{1,0:T(8,128)(2,1)}, bf16[128,2048]{1,0:T(8,128)(2,1)}) custom-call(s32[1]{0:T(128)} %bitcast.4.me_ref, bf16[128,512]{1,0:T(8,128)(2,1)S(1)} %get-tuple-element.23.refs_0_, bf16[128,512]{1,0:T(8,128)(2,1)S(1)} %collective-permute-done.7.refs_1_, bf16[128,512]{1,0:T(8,128)(2,1)S(1)} %collective-permute-done.8.refs_2_, ...), custom_call_target="tpu_custom_call" | custom-call | bytes 4194304 | tf_op jit(solution)/shard_map/join/pallas_call | solution.py:232
  (1 shorter events, 0.0 us)
Async XLA Ops:
  0.6 9.5 %copy-start = (bf16[1024,256]{1,0:T(8,128)(2,1)S(1)}, bf16[1024,256]{1,0:T(8,128)(2,1)}, u32[]{:S(2)}) copy-start(bf16[1024,256]{1,0:T(8,128)(2,1)} %refs_5_.1) | copy-start | bytes 1572868
  3.0 9.9 %copy-start.4 = (bf16[1024,256]{1,0:T(8,128)(2,1)S(1)}, bf16[1024,256]{1,0:T(8,128)(2,1)}, u32[]{:S(2)}) copy-start(bf16[1024,256]{1,0:T(8,128)(2,1)} %refs_4_.3) | copy-start | bytes 1572868
  3.0 28.5 %copy-start.2 = (bf16[1024,512]{1,0:T(8,128)(2,1)S(1)}, bf16[1024,512]{1,0:T(8,128)(2,1)}, u32[]{:S(2)}) copy-start(bf16[1024,512]{1,0:T(8,128)(2,1)} %refs_4_.2) | copy-start | bytes 3145732
  3.0 28.5 %copy-start.6 = (f32[4,1024]{1,0:T(4,128)S(1)}, f32[4,1024]{1,0:T(4,128)}, u32[]{:S(2)}) copy-start(f32[4,1024]{1,0:T(4,128)} %refs_0_.1) | copy-start | bytes 49156
  3.1 28.5 %all-to-all-start = ((bf16[8,128,512]{2,1,0:T(8,128)(2,1)}), bf16[8,128,512]{2,1,0:T(8,128)(2,1)S(1)}, u32[]{:S(2)}, u32[]{:S(2)}) async-start(bf16[8,128,512]{2,1,0:T(8,128)(2,1)} %prepare.1), calls=%async_computation | async-start | bytes 2097152 | tf_op jit(solution)/shard_map/all_to_all | solution.py:246
  10.1 9.1 %collective-permute-start.4 = (bf16[512,256]{1,0:T(8,128)(2,1)S(1)}, bf16[512,256]{1,0:T(8,128)(2,1)}, u32[]{:S(2)}, u32[]{:S(2)}) collective-permute-start(bf16[512,256]{1,0:T(8,128)(2,1)S(1)} %get-tuple-element.33), channel_id=1, source_target_pairs={{56,24},{57,25},{58,26},{59,27},{60,28},{61,29},{62,30},{63,31}} | collective-permute-start | bytes 786440 | tf_op jit(solution)/shard_map/ppermute | solution.py:267
  11.5 9.0 %collective-permute-start.2 = (bf16[512,256]{1,0:T(8,128)(2,1)S(1)}, bf16[512,256]{1,0:T(8,128)(2,1)}, u32[]{:S(2)}, u32[]{:S(2)}) collective-permute-start(bf16[512,256]{1,0:T(8,128)(2,1)S(1)} %get-tuple-element.34), channel_id=1, source_target_pairs={{56,8},{57,9},{58,10},{59,11},{60,12},{61,13},{62,14},{63,15}} | collective-permute-start | bytes 786440 | tf_op jit(solution)/shard_map/ppermute | solution.py:267
  12.9 18.7 %collective-permute-start = (bf16[1024,256]{1,0:T(8,128)(2,1)S(1)}, bf16[1024,256]{1,0:T(8,128)(2,1)}, u32[]{:S(2)}, u32[]{:S(2)}) collective-permute-start(bf16[1024,256]{1,0:T(8,128)(2,1)S(1)} %copy-done.4), channel_id=1, source_target_pairs={{0,8},{8,16},{16,24},{24,32},{32,40},{40,48},{48,56},{56,64},{64,7... | collective-permute-start | bytes 1572872 | tf_op jit(solution)/shard_map/ppermute | solution.py:159
  14.8 16.7 %collective-permute-start.1 = (bf16[1024,256]{1,0:T(8,128)(2,1)S(1)}, bf16[1024,256]{1,0:T(8,128)(2,1)}, u32[]{:S(2)}, u32[]{:S(2)}) collective-permute-start(bf16[1024,256]{1,0:T(8,128)(2,1)S(1)} %copy-done), channel_id=1, source_target_pairs={{0,8},{8,16},{16,24},{24,32},{32,40},{40,48},{48,56},{64,72},{72,8... | collective-permute-start | bytes 1572872 | tf_op jit(solution)/shard_map/ppermute | solution.py:159
  19.2 8.8 %collective-permute-start.5 = (bf16[512,256]{1,0:T(8,128)(2,1)}, bf16[512,256]{1,0:T(8,128)(2,1)S(1)}, u32[]{:S(2)}, u32[]{:S(2)}) collective-permute-start(bf16[512,256]{1,0:T(8,128)(2,1)} %collective-permute-done.4), channel_id=1, source_target_pairs={{24,64},{25,65},{26,66},{27,67},{28,68},{29,69},{30,70},{31,71}} | collective-permute-start | bytes 786440 | tf_op jit(solution)/shard_map/ppermute | solution.py:274
  20.5 8.0 %collective-permute-start.3 = (bf16[512,256]{1,0:T(8,128)(2,1)}, bf16[512,256]{1,0:T(8,128)(2,1)}, u32[]{:S(2)}, u32[]{:S(2)}) collective-permute-start(bf16[512,256]{1,0:T(8,128)(2,1)} %collective-permute-done.2), channel_id=1, source_target_pairs={{8,64},{9,65},{10,66},{11,67},{12,68},{13,69},{14,70},{15,71}} | collective-permute-start | bytes 786440 | tf_op jit(solution)/shard_map/ppermute | solution.py:274
  31.6 12.5 %copy-start.1 = (bf16[1024,256]{1,0:T(8,128)(2,1)S(1)}, bf16[1024,256]{1,0:T(8,128)(2,1)}, u32[]{:S(2)}) copy-start(bf16[1024,256]{1,0:T(8,128)(2,1)} %refs_5_.1) | copy-start | bytes 1572868
  31.6 12.5 %copy-start.3 = (bf16[1024,512]{1,0:T(8,128)(2,1)S(1)}, bf16[1024,512]{1,0:T(8,128)(2,1)}, u32[]{:S(2)}) copy-start(bf16[1024,512]{1,0:T(8,128)(2,1)} %refs_1_.3) | copy-start | bytes 3145732
  31.6 12.5 %copy-start.5 = (bf16[1024,256]{1,0:T(8,128)(2,1)S(1)}, bf16[1024,256]{1,0:T(8,128)(2,1)}, u32[]{:S(2)}) copy-start(bf16[1024,256]{1,0:T(8,128)(2,1)} %refs_4_.3) | copy-start | bytes 1572868
  42.1 17.4 %collective-permute-start.6 = (bf16[1024,512]{1,0:T(8,128)(2,1)}, bf16[1024,512]{1,0:T(8,128)(2,1)}, u32[]{:S(2)}, u32[]{:S(2)}) collective-permute-start(bf16[1024,512]{1,0:T(8,128)(2,1)} %get-tuple-element.22), channel_id=1, source_target_pairs={{8,0},{16,8},{24,16},{32,24},{40,32},{48,40},{56,48},{64,56},{72,6... | collective-permute-start | bytes 3145736 | tf_op jit(solution)/shard_map/ppermute | solution.py:159
  53.1 31.4 %all-to-all-start.1 = ((bf16[8,128,512]{2,1,0:T(8,128)(2,1)}), bf16[8,128,512]{2,1,0:T(8,128)(2,1)}, u32[]{:S(2)}, u32[]{:S(2)}) async-start(bf16[8,128,512]{2,1,0:T(8,128)(2,1)} %bitcast.9), calls=%async_computation.1 | async-start | bytes 2097152 | tf_op jit(solution)/shard_map/all_to_all | solution.py:246
  60.9 17.5 %collective-permute-start.7 = (bf16[128,512]{1,0:T(8,128)(2,1)S(1)}, bf16[128,512]{1,0:T(8,128)(2,1)S(1)}, u32[]{:S(2)}, u32[]{:S(2)}) collective-permute-start(bf16[128,512]{1,0:T(8,128)(2,1)S(1)} %get-tuple-element.24), channel_id=1, source_target_pairs={{0,2},{1,3},{2,4},{3,5},{4,6},{5,7},{6,0},{7,1},{8,10},{9,11},{10,... | collective-permute-start | bytes 393224 | tf_op jit(solution)/shard_map/ppermute | solution.py:255
  63.0 20.3 %collective-permute-start.8 = (bf16[128,512]{1,0:T(8,128)(2,1)S(1)}, bf16[128,512]{1,0:T(8,128)(2,1)S(1)}, u32[]{:S(2)}, u32[]{:S(2)}) collective-permute-start(bf16[128,512]{1,0:T(8,128)(2,1)S(1)} %get-tuple-element.25), channel_id=1, source_target_pairs={{0,1},{1,0},{2,3},{3,2},{4,5},{5,4},{6,7},{7,6},{8,9},{9,8},{10,11... | collective-permute-start | bytes 393224 | tf_op jit(solution)/shard_map/ppermute | solution.py:255
  65.9 21.0 %collective-permute-start.9 = (bf16[128,512]{1,0:T(8,128)(2,1)S(1)}, bf16[128,512]{1,0:T(8,128)(2,1)S(1)}, u32[]{:S(2)}, u32[]{:S(2)}) collective-permute-start(bf16[128,512]{1,0:T(8,128)(2,1)S(1)} %get-tuple-element.26), channel_id=1, source_target_pairs={{0,6},{1,7},{2,0},{3,1},{4,2},{5,3},{6,4},{7,5},{8,14},{9,15},{10,... | collective-permute-start | bytes 393224 | tf_op jit(solution)/shard_map/ppermute | solution.py:255
  67.7 19.2 %collective-permute-start.10 = (bf16[128,512]{1,0:T(8,128)(2,1)S(1)}, bf16[128,512]{1,0:T(8,128)(2,1)S(1)}, u32[]{:S(2)}, u32[]{:S(2)}) collective-permute-start(bf16[128,512]{1,0:T(8,128)(2,1)S(1)} %get-tuple-element.27), channel_id=1, source_target_pairs={{0,5},{1,4},{2,7},{3,6},{4,1},{5,0},{6,3},{7,2},{8,13},{9,12},{10,... | collective-permute-start | bytes 393224 | tf_op jit(solution)/shard_map/ppermute | solution.py:255
  69.5 17.4 %collective-permute-start.11 = (bf16[128,512]{1,0:T(8,128)(2,1)S(1)}, bf16[128,512]{1,0:T(8,128)(2,1)S(1)}, u32[]{:S(2)}, u32[]{:S(2)}) collective-permute-start(bf16[128,512]{1,0:T(8,128)(2,1)S(1)} %get-tuple-element.28), channel_id=1, source_target_pairs={{0,4},{1,5},{2,6},{3,7},{4,0},{5,1},{6,2},{7,3},{8,12},{9,13},{10,... | collective-permute-start | bytes 393224 | tf_op jit(solution)/shard_map/ppermute | solution.py:255
  78.4 9.5 %collective-permute-start.12 = (bf16[128,512]{1,0:T(8,128)(2,1)S(1)}, bf16[128,512]{1,0:T(8,128)(2,1)S(1)}, u32[]{:S(2)}, u32[]{:S(2)}) collective-permute-start(bf16[128,512]{1,0:T(8,128)(2,1)S(1)} %get-tuple-element.29), channel_id=1, source_target_pairs={{0,3},{1,2},{2,5},{3,4},{4,7},{5,6},{6,1},{7,0},{8,11},{9,10},{10,... | collective-permute-start | bytes 393224 | tf_op jit(solution)/shard_map/ppermute | solution.py:255
  83.2 7.4 %collective-permute-start.13 = (bf16[128,512]{1,0:T(8,128)(2,1)S(1)}, bf16[128,512]{1,0:T(8,128)(2,1)S(1)}, u32[]{:S(2)}, u32[]{:S(2)}) collective-permute-start(bf16[128,512]{1,0:T(8,128)(2,1)S(1)} %get-tuple-element.30), channel_id=1, source_target_pairs={{0,7},{1,6},{2,1},{3,0},{4,3},{5,2},{6,5},{7,4},{8,15},{9,14},{10,... | collective-permute-start | bytes 393224 | tf_op jit(solution)/shard_map/ppermute | solution.py:255

commit v4 on v3

--- a/solution.py
+++ b/solution.py
@@ -146,7 +146,7 @@
         out_specs=out_specs,
         out_shape=out_shape,
         scratch_shapes=scratch,
-        compiler_params=pltpu.CompilerParams(vmem_limit_bytes=24000 * 1024),
+        compiler_params=pltpu.CompilerParams(vmem_limit_bytes=20000 * 1024),
         cost_estimate=pl.CostEstimate(
             flops=4 * 10**9, bytes_accessed=8 * 2**20, transcendentals=3 * 10**6
         ),
@@ -188,7 +188,7 @@
     )(out_grad)
 
 
-HOPS = [(0, 0), (1, 0), (0, 1), (3, 0), (2, 1), (2, 0), (1, 1), (3, 1)]
+HOPS = [(0, 0), (1, 0), (2, 1), (0, 1), (3, 0), (1, 1), (2, 0), (3, 1)]
 
 
 def sum_kernel(me_ref, own_ref, later_ref, *out_refs):
@@ -209,7 +209,7 @@
         in_specs=[pl.BlockSpec(memory_space=pltpu.SMEM), vmem, vmem],
         out_specs=[vmem] * members,
         out_shape=[jax.ShapeDtypeStruct((rows, 2 * PAIR), jnp.bfloat16)] * members,
-        compiler_params=pltpu.CompilerParams(vmem_limit_bytes=16 * 2**20),
+        compiler_params=pltpu.CompilerParams(vmem_limit_bytes=6 * 2**20),
         cost_estimate=pl.CostEstimate(flops=10**6, bytes_accessed=4 * 2**20, transcendentals=0),
     )(me, own, later)
 

time: 93.3 us -> 92.6 us (level)
  waiting for transfers between devices: 21.1 us -> 17.8 us
  starting transfers between devices: 42.9 us -> 46.1 us
    ppermute x7, waiting for transfers between devices: 11.4 us -> 8.09 us  [shift_heads(): return lax.ppermute(x, 'head', [(i, partner(i, hop)) for i in range(8)])]
    ppermute x7, starting transfers between devices: 16 us -> 19.2 us  [shift_heads(): return lax.ppermute(x, 'head', [(i, partner(i, hop)) for i in range(8)])]
where the time goes in v4:
time: 92.6 us; the launch traced here: 91.7 us
  starting transfers between devices  46.1 us (50%)
  Pallas kernels  24.6 us (27%)
  waiting for transfers between devices  17.8 us (19%)
  local copies, waits for them, and re-layouts  2.39 us (3%)
    pallas_call x2, Pallas kernels, band(): pl.pallas_call(functools.partial(band_kernel, own), name='own_band' if ow...  19.6 us
    ppermute x7, starting transfers between devices, shift_heads(): return lax.ppermute(x, 'head', [(i, partner(i, hop)) for i in range(8)])  19.2 us
    all_to_all x2, starting transfers between devices, exchange(): lax.all_to_all(parts, 'head', split_axis=0, concat_axis=0, tiled=True)  13.3 us
    ppermute x3, starting transfers between devices, from_behind(): return lax.ppermute(shard, 'seq', pairs)  8.23 us
    ppermute x7, waiting for transfers between devices, shift_heads(): return lax.ppermute(x, 'head', [(i, partner(i, hop)) for i in range(8)])  8.09 us
    ppermute x2, waiting for transfers between devices, on_device(): v_far.append(lax.ppermute(detours[n], 'seq', [(middle[n], half)]))  6.7 us
    ppermute x3, waiting for transfers between devices, from_behind(): return lax.ppermute(shard, 'seq', pairs)  3.02 us
    ppermute x2, starting transfers between devices, on_device(): detours.append(lax.ppermute(rows, 'seq', [(half - 1, middle[n])]))  2.75 us
  transfers between devices with their start and end apart: 16, of which 6 were waited for; matrix products, arithmetic and copies ran while one was open for 3% of the time, Pallas kernels for 11%

profile of v4, /device:TPU:2, one launch (start us, length us, event | category | flops | bytes accessed | tf_op | source)
XLA Modules:
  0.0 91.7 jit_solution(16283586685829183391)
XLA Ops:
  0.6 0.0 copy-start
  0.6 2.4 %prepare.1 = bf16[8,128,512]{2,1,0:T(8,128)(2,1)} custom-call(bf16[128,4096]{1,0:T(8,128)(2,1)} %g_ref.1), custom_call_target="tpu_custom_call" | custom-call | bytes 2097152 | tf_op jit(solution)/shard_map/prepare/pallas_call | solution.py:178
  3.0 0.0 copy-start.4
  3.0 0.0 copy-start.2
  3.0 0.0 copy-start.6
  3.1 7.0 %all-to-all-start = ((bf16[8,128,512]{2,1,0:T(8,128)(2,1)}), bf16[8,128,512]{2,1,0:T(8,128)(2,1)S(1)}, u32[]{:S(2)}, u32[]{:S(2)}) async-start(bf16[8,128,512]{2,1,0:T(8,128)(2,1)} %prepare.1), calls=%async_computation | async-start | bytes 2097152 | tf_op jit(solution)/shard_map/all_to_all | solution.py:246
  10.1 0.0 copy-done
  10.1 1.4 %collective-permute-start.4 = (bf16[512,256]{1,0:T(8,128)(2,1)S(1)}, bf16[512,256]{1,0:T(8,128)(2,1)}, u32[]{:S(2)}, u32[]{:S(2)}) collective-permute-start(bf16[512,256]{1,0:T(8,128)(2,1)S(1)} %get-tuple-element.33), channel_id=1, source_target_pairs={{56,24},{57,25},{58,26},{59,27},{60,28},{61,29},{62,30},{63,31}} | collective-permute-start | bytes 786440 | tf_op jit(solution)/shard_map/ppermute | solution.py:267
  11.5 1.4 %collective-permute-start.2 = (bf16[512,256]{1,0:T(8,128)(2,1)S(1)}, bf16[512,256]{1,0:T(8,128)(2,1)}, u32[]{:S(2)}, u32[]{:S(2)}) collective-permute-start(bf16[512,256]{1,0:T(8,128)(2,1)S(1)} %get-tuple-element.34), channel_id=1, source_target_pairs={{56,8},{57,9},{58,10},{59,11},{60,12},{61,13},{62,14},{63,15}} | collective-permute-start | bytes 786440 | tf_op jit(solution)/shard_map/ppermute | solution.py:267
  12.9 0.0 copy-done.4
  12.9 1.9 %collective-permute-start = (bf16[1024,256]{1,0:T(8,128)(2,1)S(1)}, bf16[1024,256]{1,0:T(8,128)(2,1)}, u32[]{:S(2)}, u32[]{:S(2)}) collective-permute-start(bf16[1024,256]{1,0:T(8,128)(2,1)S(1)} %copy-done.4), channel_id=1, source_target_pairs={{0,8},{8,16},{16,24},{24,32},{32,40},{40,48},{48,56},{56,64},{64,7... | collective-permute-start | bytes 1572872 | tf_op jit(solution)/shard_map/ppermute | solution.py:159
  14.8 4.4 %collective-permute-start.1 = (bf16[1024,256]{1,0:T(8,128)(2,1)S(1)}, bf16[1024,256]{1,0:T(8,128)(2,1)}, u32[]{:S(2)}, u32[]{:S(2)}) collective-permute-start(bf16[1024,256]{1,0:T(8,128)(2,1)S(1)} %copy-done), channel_id=1, source_target_pairs={{0,8},{8,16},{16,24},{24,32},{32,40},{40,48},{48,56},{64,72},{72,8... | collective-permute-start | bytes 1572872 | tf_op jit(solution)/shard_map/ppermute | solution.py:159
  19.2 0.0 collective-permute-done.4
  19.2 1.3 %collective-permute-start.5 = (bf16[512,256]{1,0:T(8,128)(2,1)}, bf16[512,256]{1,0:T(8,128)(2,1)S(1)}, u32[]{:S(2)}, u32[]{:S(2)}) collective-permute-start(bf16[512,256]{1,0:T(8,128)(2,1)} %collective-permute-done.4), channel_id=1, source_target_pairs={{24,64},{25,65},{26,66},{27,67},{28,68},{29,69},{30,70},{31,71}} | collective-permute-start | bytes 786440 | tf_op jit(solution)/shard_map/ppermute | solution.py:274
  20.5 0.0 collective-permute-done.2
  20.5 1.3 %collective-permute-start.3 = (bf16[512,256]{1,0:T(8,128)(2,1)}, bf16[512,256]{1,0:T(8,128)(2,1)}, u32[]{:S(2)}, u32[]{:S(2)}) collective-permute-start(bf16[512,256]{1,0:T(8,128)(2,1)} %collective-permute-done.2), channel_id=1, source_target_pairs={{8,64},{9,65},{10,66},{11,67},{12,68},{13,69},{14,70},{15,71}} | collective-permute-start | bytes 786440 | tf_op jit(solution)/shard_map/ppermute | solution.py:274
  21.8 6.2 %collective-permute-done.5.refs_8_ = bf16[512,256]{1,0:T(8,128)(2,1)S(1)} collective-permute-done((bf16[512,256]{1,0:T(8,128)(2,1)}, bf16[512,256]{1,0:T(8,128)(2,1)S(1)}, u32[]{:S(2)}, u32[]{:S(2)}) %collective-permute-start.5) | collective-permute-done | bytes 262176 | tf_op jit(solution)/shard_map/ppermute | solution.py:274
  28.0 0.5 collective-permute-done.3.refs_7_
  28.5 3.0 %collective-permute-done.refs_5_ = bf16[1024,256]{1,0:T(8,128)(2,1)} collective-permute-done((bf16[1024,256]{1,0:T(8,128)(2,1)S(1)}, bf16[1024,256]{1,0:T(8,128)(2,1)}, u32[]{:S(2)}, u32[]{:S(2)}) %collective-permute-start) | collective-permute-done | bytes 524320 | tf_op jit(solution)/shard_map/ppermute | solution.py:159
  31.5 0.0 collective-permute-done.1.refs_6_
  31.5 0.0 all-to-all-done
  31.5 0.0 copy-done.2
  31.5 0.0 copy-done.6
  31.6 0.0 copy-start.1
  31.6 0.0 copy-start.3
  31.6 0.0 copy-start.5
  31.6 10.5 %rim_band.1 = (f32[512,1024]{1,0:T(8,128)S(1)}, bf16[1024,512]{1,0:T(8,128)(2,1)}, f32[32,1024]{1,0:T(8,128)S(1)}) custom-call(f32[1]{0:T(128)} %bitcast.1.refs_0_, f32[4,1024]{1,0:T(4,128)S(1)} %copy-done.6, bf16[1024,512]{1,0:T(8,128)(2,1)} %refs_1_.3, bf16[1024,512]{1,0:T(8,128)(2,1)S(1)} %bitcast.7, bf16[1024,512]{1,0:T(8,128)(2,1)S(1)} %copy-done.2, ...), custom_call_target="tpu_custom_call" | custom-call | flops 4000000000 | bytes 8388608 | tf_op jit(solution)/shard_map/rim_band/pallas_call | solution.py:141
  42.1 1.9 %collective-permute-start.6 = (bf16[1024,512]{1,0:T(8,128)(2,1)}, bf16[1024,512]{1,0:T(8,128)(2,1)}, u32[]{:S(2)}, u32[]{:S(2)}) collective-permute-start(bf16[1024,512]{1,0:T(8,128)(2,1)} %get-tuple-element.22), channel_id=1, source_target_pairs={{8,0},{16,8},{24,16},{32,24},{40,32},{48,40},{56,48},{64,56},{72,6... | collective-permute-start | bytes 3145736 | tf_op jit(solution)/shard_map/ppermute | solution.py:159
  44.0 0.0 copy-done.1
  44.0 0.0 copy-done.3
  44.0 0.0 copy-done.5
  44.1 9.1 %own_band.1 = (bf16[1024,512]{1,0:T(8,128)(2,1)}, f32[1024,512]{1,0:T(8,128)S(1)}) custom-call(f32[4,1024]{1,0:T(4,128)S(1)} %copy-done.6, bf16[1024,512]{1,0:T(8,128)(2,1)S(1)} %copy-done.3, bf16[1024,512]{1,0:T(8,128)(2,1)S(1)} %bitcast.8, f32[32,1024]{1,0:T(8,128)S(1)} %get-tuple-element.18.refs_3_, bf16[1024,256]{1,0:T(8,128)(2,1)S(1)} %copy-done.5, ...), custom_call_target="tpu_custom_call" | custom-call | flops 4000000000 | bytes 8388608 | tf_op jit(solution)/shard_map/own_band/pallas_call | solution.py:141
  53.1 6.3 %all-to-all-start.1 = ((bf16[8,128,512]{2,1,0:T(8,128)(2,1)}), bf16[8,128,512]{2,1,0:T(8,128)(2,1)}, u32[]{:S(2)}, u32[]{:S(2)}) async-start(bf16[8,128,512]{2,1,0:T(8,128)(2,1)} %bitcast.9), calls=%async_computation.1 | async-start | bytes 2097152 | tf_op jit(solution)/shard_map/all_to_all | solution.py:246
  59.5 0.0 collective-permute-done.6.later_ref
  59.5 1.4 %sum_parts.1 = (bf16[128,512]{1,0:T(8,128)(2,1)S(1)}, bf16[128,512]{1,0:T(8,128)(2,1)S(1)}, bf16[128,512]{1,0:T(8,128)(2,1)S(1)}, bf16[128,512]{1,0:T(8,128)(2,1...) custom-call(s32[1]{0:T(128)} %bitcast.4.me_ref, ...), custom_call_target="tpu_custom_call" | custom-call | flops 1000000 | bytes 4194304 | tf_op jit(solution)/shard_map/sum_parts/pallas_call | solution.py:206
  60.9 2.1 %collective-permute-start.7 = (bf16[128,512]{1,0:T(8,128)(2,1)S(1)}, bf16[128,512]{1,0:T(8,128)(2,1)S(1)}, u32[]{:S(2)}, u32[]{:S(2)}) collective-permute-start(bf16[128,512]{1,0:T(8,128)(2,1)S(1)} %get-tuple-element.24), channel_id=1, source_target_pairs={{0,2},{1,3},{2,4},{3,5},{4,6},{5,7},{6,0},{7,1},{8,10},{9,11},{10,... | collective-permute-start | bytes 393224 | tf_op jit(solution)/shard_map/ppermute | solution.py:255
  63.0 5.1 %collective-permute-start.8 = (bf16[128,512]{1,0:T(8,128)(2,1)S(1)}, bf16[128,512]{1,0:T(8,128)(2,1)S(1)}, u32[]{:S(2)}, u32[]{:S(2)}) collective-permute-start(bf16[128,512]{1,0:T(8,128)(2,1)S(1)} %get-tuple-element.25), channel_id=1, source_target_pairs={{0,5},{1,4},{2,7},{3,6},{4,1},{5,0},{6,3},{7,2},{8,13},{9,12},{10,... | collective-permute-start | bytes 393224 | tf_op jit(solution)/shard_map/ppermute | solution.py:255
  68.0 0.6 collective-permute-start.9
  68.6 1.5 %collective-permute-start.10 = (bf16[128,512]{1,0:T(8,128)(2,1)S(1)}, bf16[128,512]{1,0:T(8,128)(2,1)S(1)}, u32[]{:S(2)}, u32[]{:S(2)}) collective-permute-start(bf16[128,512]{1,0:T(8,128)(2,1)S(1)} %get-tuple-element.27), channel_id=1, source_target_pairs={{0,6},{1,7},{2,0},{3,1},{4,2},{5,3},{6,4},{7,5},{8,14},{9,15},{10,... | collective-permute-start | bytes 393224 | tf_op jit(solution)/shard_map/ppermute | solution.py:255
  70.1 3.0 %collective-permute-start.11 = (bf16[128,512]{1,0:T(8,128)(2,1)S(1)}, bf16[128,512]{1,0:T(8,128)(2,1)S(1)}, u32[]{:S(2)}, u32[]{:S(2)}) collective-permute-start(bf16[128,512]{1,0:T(8,128)(2,1)S(1)} %get-tuple-element.28), channel_id=1, source_target_pairs={{0,3},{1,2},{2,5},{3,4},{4,7},{5,6},{6,1},{7,0},{8,11},{9,10},{10,... | collective-permute-start | bytes 393224 | tf_op jit(solution)/shard_map/ppermute | solution.py:255
  73.0 4.3 %collective-permute-done.7.refs_1_ = bf16[128,512]{1,0:T(8,128)(2,1)S(1)} collective-permute-done((bf16[128,512]{1,0:T(8,128)(2,1)S(1)}, bf16[128,512]{1,0:T(8,128)(2,1)S(1)}, u32[]{:S(2)}, u32[]{:S(2)}) %collective-permute-start.7) | collective-permute-done | bytes 131104 | tf_op jit(solution)/shard_map/ppermute | solution.py:255
  77.3 0.9 collective-permute-start.12
  78.2 3.6 %collective-permute-done.8.refs_2_ = bf16[128,512]{1,0:T(8,128)(2,1)S(1)} collective-permute-done((bf16[128,512]{1,0:T(8,128)(2,1)S(1)}, bf16[128,512]{1,0:T(8,128)(2,1)S(1)}, u32[]{:S(2)}, u32[]{:S(2)}) %collective-permute-start.8) | collective-permute-done | bytes 131104 | tf_op jit(solution)/shard_map/ppermute | solution.py:255
  81.8 6.2 %collective-permute-start.13 = (bf16[128,512]{1,0:T(8,128)(2,1)S(1)}, bf16[128,512]{1,0:T(8,128)(2,1)S(1)}, u32[]{:S(2)}, u32[]{:S(2)}) collective-permute-start(bf16[128,512]{1,0:T(8,128)(2,1)S(1)} %get-tuple-element.30), channel_id=1, source_target_pairs={{0,7},{1,6},{2,1},{3,0},{4,3},{5,2},{6,5},{7,4},{8,15},{9,14},{10,... | collective-permute-start | bytes 393224 | tf_op jit(solution)/shard_map/ppermute | solution.py:255
  88.0 0.0 all-to-all-done.1
  88.0 2.3 %copy.10 = bf16[8,16,8,512]{3,2,0,1:T(8,128)(2,1)} copy(bf16[8,16,8,512]{3,2,1,0:T(8,128)(2,1)} %bitcast.5) | data formatting | bytes 2097152 | tf_op jit(solution)/shard_map/reshape | solution.py:285
  90.3 0.0 collective-permute-done.9.refs_3_
  90.3 0.0 collective-permute-done.10.refs_4_
  90.3 0.0 collective-permute-done.11.refs_5_
  90.3 0.0 collective-permute-done.12.refs_6_
  90.3 0.2 collective-permute-done.13.refs_7_
  90.5 1.3 %join.1 = (bf16[128,2048]{1,0:T(8,128)(2,1)}, bf16[128,2048]{1,0:T(8,128)(2,1)}) custom-call(s32[1]{0:T(128)} %bitcast.4.me_ref, bf16[128,512]{1,0:T(8,128)(2,1)S(1)} %get-tuple-element.23.refs_0_, bf16[128,512]{1,0:T(8,128)(2,1)S(1)} %collective-permute-done.7.refs_1_, bf16[128,512]{1,0:T(8,128)(2,1)S(1)} %collective-permute-done.8.refs_2_, ...), custom_call_target="tpu_custom_call" | custom-call | bytes 4194304 | tf_op jit(solution)/shard_map/join/pallas_call | solution.py:232
  (1 shorter events, 0.0 us)
Async XLA Ops:
  0.6 9.5 %copy-start = (bf16[1024,256]{1,0:T(8,128)(2,1)S(1)}, bf16[1024,256]{1,0:T(8,128)(2,1)}, u32[]{:S(2)}) copy-start(bf16[1024,256]{1,0:T(8,128)(2,1)} %refs_5_.1) | copy-start | bytes 1572868
  3.0 9.9 %copy-start.4 = (bf16[1024,256]{1,0:T(8,128)(2,1)S(1)}, bf16[1024,256]{1,0:T(8,128)(2,1)}, u32[]{:S(2)}) copy-start(bf16[1024,256]{1,0:T(8,128)(2,1)} %refs_4_.3) | copy-start | bytes 1572868
  3.0 28.5 %copy-start.2 = (bf16[1024,512]{1,0:T(8,128)(2,1)S(1)}, bf16[1024,512]{1,0:T(8,128)(2,1)}, u32[]{:S(2)}) copy-start(bf16[1024,512]{1,0:T(8,128)(2,1)} %refs_4_.2) | copy-start | bytes 3145732
  3.0 28.5 %copy-start.6 = (f32[4,1024]{1,0:T(4,128)S(1)}, f32[4,1024]{1,0:T(4,128)}, u32[]{:S(2)}) copy-start(f32[4,1024]{1,0:T(4,128)} %refs_0_.1) | copy-start | bytes 49156
  3.1 28.5 %all-to-all-start = ((bf16[8,128,512]{2,1,0:T(8,128)(2,1)}), bf16[8,128,512]{2,1,0:T(8,128)(2,1)S(1)}, u32[]{:S(2)}, u32[]{:S(2)}) async-start(bf16[8,128,512]{2,1,0:T(8,128)(2,1)} %prepare.1), calls=%async_computation | async-start | bytes 2097152 | tf_op jit(solution)/shard_map/all_to_all | solution.py:246
  10.1 9.1 %collective-permute-start.4 = (bf16[512,256]{1,0:T(8,128)(2,1)S(1)}, bf16[512,256]{1,0:T(8,128)(2,1)}, u32[]{:S(2)}, u32[]{:S(2)}) collective-permute-start(bf16[512,256]{1,0:T(8,128)(2,1)S(1)} %get-tuple-element.33), channel_id=1, source_target_pairs={{56,24},{57,25},{58,26},{59,27},{60,28},{61,29},{62,30},{63,31}} | collective-permute-start | bytes 786440 | tf_op jit(solution)/shard_map/ppermute | solution.py:267
  11.5 9.0 %collective-permute-start.2 = (bf16[512,256]{1,0:T(8,128)(2,1)S(1)}, bf16[512,256]{1,0:T(8,128)(2,1)}, u32[]{:S(2)}, u32[]{:S(2)}) collective-permute-start(bf16[512,256]{1,0:T(8,128)(2,1)S(1)} %get-tuple-element.34), channel_id=1, source_target_pairs={{56,8},{57,9},{58,10},{59,11},{60,12},{61,13},{62,14},{63,15}} | collective-permute-start | bytes 786440 | tf_op jit(solution)/shard_map/ppermute | solution.py:267
  12.9 18.7 %collective-permute-start = (bf16[1024,256]{1,0:T(8,128)(2,1)S(1)}, bf16[1024,256]{1,0:T(8,128)(2,1)}, u32[]{:S(2)}, u32[]{:S(2)}) collective-permute-start(bf16[1024,256]{1,0:T(8,128)(2,1)S(1)} %copy-done.4), channel_id=1, source_target_pairs={{0,8},{8,16},{16,24},{24,32},{32,40},{40,48},{48,56},{56,64},{64,7... | collective-permute-start | bytes 1572872 | tf_op jit(solution)/shard_map/ppermute | solution.py:159
  14.8 16.7 %collective-permute-start.1 = (bf16[1024,256]{1,0:T(8,128)(2,1)S(1)}, bf16[1024,256]{1,0:T(8,128)(2,1)}, u32[]{:S(2)}, u32[]{:S(2)}) collective-permute-start(bf16[1024,256]{1,0:T(8,128)(2,1)S(1)} %copy-done), channel_id=1, source_target_pairs={{0,8},{8,16},{16,24},{24,32},{32,40},{40,48},{48,56},{64,72},{72,8... | collective-permute-start | bytes 1572872 | tf_op jit(solution)/shard_map/ppermute | solution.py:159
  19.2 8.8 %collective-permute-start.5 = (bf16[512,256]{1,0:T(8,128)(2,1)}, bf16[512,256]{1,0:T(8,128)(2,1)S(1)}, u32[]{:S(2)}, u32[]{:S(2)}) collective-permute-start(bf16[512,256]{1,0:T(8,128)(2,1)} %collective-permute-done.4), channel_id=1, source_target_pairs={{24,64},{25,65},{26,66},{27,67},{28,68},{29,69},{30,70},{31,71}} | collective-permute-start | bytes 786440 | tf_op jit(solution)/shard_map/ppermute | solution.py:274
  20.5 8.0 %collective-permute-start.3 = (bf16[512,256]{1,0:T(8,128)(2,1)}, bf16[512,256]{1,0:T(8,128)(2,1)}, u32[]{:S(2)}, u32[]{:S(2)}) collective-permute-start(bf16[512,256]{1,0:T(8,128)(2,1)} %collective-permute-done.2), channel_id=1, source_target_pairs={{8,64},{9,65},{10,66},{11,67},{12,68},{13,69},{14,70},{15,71}} | collective-permute-start | bytes 786440 | tf_op jit(solution)/shard_map/ppermute | solution.py:274
  31.6 12.5 %copy-start.1 = (bf16[1024,256]{1,0:T(8,128)(2,1)S(1)}, bf16[1024,256]{1,0:T(8,128)(2,1)}, u32[]{:S(2)}) copy-start(bf16[1024,256]{1,0:T(8,128)(2,1)} %refs_5_.1) | copy-start | bytes 1572868
  31.6 12.5 %copy-start.3 = (bf16[1024,512]{1,0:T(8,128)(2,1)S(1)}, bf16[1024,512]{1,0:T(8,128)(2,1)}, u32[]{:S(2)}) copy-start(bf16[1024,512]{1,0:T(8,128)(2,1)} %refs_1_.3) | copy-start | bytes 3145732
  31.6 12.5 %copy-start.5 = (bf16[1024,256]{1,0:T(8,128)(2,1)S(1)}, bf16[1024,256]{1,0:T(8,128)(2,1)}, u32[]{:S(2)}) copy-start(bf16[1024,256]{1,0:T(8,128)(2,1)} %refs_4_.3) | copy-start | bytes 1572868
  42.1 17.4 %collective-permute-start.6 = (bf16[1024,512]{1,0:T(8,128)(2,1)}, bf16[1024,512]{1,0:T(8,128)(2,1)}, u32[]{:S(2)}, u32[]{:S(2)}) collective-permute-start(bf16[1024,512]{1,0:T(8,128)(2,1)} %get-tuple-element.22), channel_id=1, source_target_pairs={{8,0},{16,8},{24,16},{32,24},{40,32},{48,40},{56,48},{64,56},{72,6... | collective-permute-start | bytes 3145736 | tf_op jit(solution)/shard_map/ppermute | solution.py:159
  53.1 34.8 %all-to-all-start.1 = ((bf16[8,128,512]{2,1,0:T(8,128)(2,1)}), bf16[8,128,512]{2,1,0:T(8,128)(2,1)}, u32[]{:S(2)}, u32[]{:S(2)}) async-start(bf16[8,128,512]{2,1,0:T(8,128)(2,1)} %bitcast.9), calls=%async_computation.1 | async-start | bytes 2097152 | tf_op jit(solution)/shard_map/all_to_all | solution.py:246
  60.9 16.4 %collective-permute-start.7 = (bf16[128,512]{1,0:T(8,128)(2,1)S(1)}, bf16[128,512]{1,0:T(8,128)(2,1)S(1)}, u32[]{:S(2)}, u32[]{:S(2)}) collective-permute-start(bf16[128,512]{1,0:T(8,128)(2,1)S(1)} %get-tuple-element.24), channel_id=1, source_target_pairs={{0,2},{1,3},{2,4},{3,5},{4,6},{5,7},{6,0},{7,1},{8,10},{9,11},{10,... | collective-permute-start | bytes 393224 | tf_op jit(solution)/shard_map/ppermute | solution.py:255
  63.0 18.8 %collective-permute-start.8 = (bf16[128,512]{1,0:T(8,128)(2,1)S(1)}, bf16[128,512]{1,0:T(8,128)(2,1)S(1)}, u32[]{:S(2)}, u32[]{:S(2)}) collective-permute-start(bf16[128,512]{1,0:T(8,128)(2,1)S(1)} %get-tuple-element.25), channel_id=1, source_target_pairs={{0,5},{1,4},{2,7},{3,6},{4,1},{5,0},{6,3},{7,2},{8,13},{9,12},{10,... | collective-permute-start | bytes 393224 | tf_op jit(solution)/shard_map/ppermute | solution.py:255
  68.0 22.2 %collective-permute-start.9 = (bf16[128,512]{1,0:T(8,128)(2,1)S(1)}, bf16[128,512]{1,0:T(8,128)(2,1)S(1)}, u32[]{:S(2)}, u32[]{:S(2)}) collective-permute-start(bf16[128,512]{1,0:T(8,128)(2,1)S(1)} %get-tuple-element.26), channel_id=1, source_target_pairs={{0,1},{1,0},{2,3},{3,2},{4,5},{5,4},{6,7},{7,6},{8,9},{9,8},{10,11... | collective-permute-start | bytes 393224 | tf_op jit(solution)/shard_map/ppermute | solution.py:255
  68.6 21.7 %collective-permute-start.10 = (bf16[128,512]{1,0:T(8,128)(2,1)S(1)}, bf16[128,512]{1,0:T(8,128)(2,1)S(1)}, u32[]{:S(2)}, u32[]{:S(2)}) collective-permute-start(bf16[128,512]{1,0:T(8,128)(2,1)S(1)} %get-tuple-element.27), channel_id=1, source_target_pairs={{0,6},{1,7},{2,0},{3,1},{4,2},{5,3},{6,4},{7,5},{8,14},{9,15},{10,... | collective-permute-start | bytes 393224 | tf_op jit(solution)/shard_map/ppermute | solution.py:255
  70.1 20.2 %collective-permute-start.11 = (bf16[128,512]{1,0:T(8,128)(2,1)S(1)}, bf16[128,512]{1,0:T(8,128)(2,1)S(1)}, u32[]{:S(2)}, u32[]{:S(2)}) collective-permute-start(bf16[128,512]{1,0:T(8,128)(2,1)S(1)} %get-tuple-element.28), channel_id=1, source_target_pairs={{0,3},{1,2},{2,5},{3,4},{4,7},{5,6},{6,1},{7,0},{8,11},{9,10},{10,... | collective-permute-start | bytes 393224 | tf_op jit(solution)/shard_map/ppermute | solution.py:255
  77.3 13.0 %collective-permute-start.12 = (bf16[128,512]{1,0:T(8,128)(2,1)S(1)}, bf16[128,512]{1,0:T(8,128)(2,1)S(1)}, u32[]{:S(2)}, u32[]{:S(2)}) collective-permute-start(bf16[128,512]{1,0:T(8,128)(2,1)S(1)} %get-tuple-element.29), channel_id=1, source_target_pairs={{0,4},{1,5},{2,6},{3,7},{4,0},{5,1},{6,2},{7,3},{8,12},{9,13},{10,... | collective-permute-start | bytes 393224 | tf_op jit(solution)/shard_map/ppermute | solution.py:255
  81.8 8.7 %collective-permute-start.13 = (bf16[128,512]{1,0:T(8,128)(2,1)S(1)}, bf16[128,512]{1,0:T(8,128)(2,1)S(1)}, u32[]{:S(2)}, u32[]{:S(2)}) collective-permute-start(bf16[128,512]{1,0:T(8,128)(2,1)S(1)} %get-tuple-element.30), channel_id=1, source_target_pairs={{0,7},{1,6},{2,1},{3,0},{4,3},{5,2},{6,5},{7,4},{8,15},{9,14},{10,... | collective-permute-start | bytes 393224 | tf_op jit(solution)/shard_map/ppermute | solution.py:255
